TPU v7x, 128 devices: a whole 4x4x4 slice. The times are simulated.
128 devices in a mesh: pipe: 4 (over x_hi, core), dp: 32 (over y, z, x_lo).
Axes of the slice: x: 4 (x_hi: 2, x_lo: 2; x = x_hi * 2 + x_lo), y: 4, z: 4, core: 2. Of those that a mesh axis runs over, the one named last changes fastest.
Arguments:
- layer_input: bfloat16 [4, 4096, 8192], P('pipe', 'dp'), may hold values from -130 to 130
- queries: bfloat16 [4, 4096, 4096], P('pipe', 'dp'), may hold values from -35 to 35
- out_grad: bfloat16 [4, 4096, 4096], P('pipe', 'dp'), may hold values from -6 to 6
- top_grad: bfloat16 [4096, 8192], P('dp'), may hold values from -4 to 4
- norm_gain: bfloat16 [4, 8192], P('pipe', 'dp'), may hold values from 0.5 to 1.5
- key_weight: bfloat16 [4, 8192, 512], P('pipe', 'dp'), may hold values from -0.0625 to 0.0625
- value_weight: bfloat16 [4, 8192, 512], P('pipe', 'dp'), may hold values from -0.0625 to 0.0625
- weight_exponents: int32 [4, 2, 64, 4], P('pipe', None, 'dp'), may hold values from -1 to 1
- doc_lengths: int32 [64], replicated, may hold values from 1 to 512, 4096 in all
Outputs:
- input_grad: bfloat16 [4, 4096, 8192], P('pipe', 'dp')
- query_grad: bfloat16 [4, 4096, 4096], P('pipe', 'dp')
- key_weight_grad: float32 [4, 8192, 512], P('pipe', 'dp')
- value_weight_grad: float32 [4, 8192, 512], P('pipe', 'dp')
- gain_grad: float32 [4, 8192], P('pipe', 'dp')
Inputs may be any that keep to these rules, and one draw needn't show every extreme that they name: `doc_lengths`: the lengths sum to 4096; the longest is exactly 512. `weight_exponents`: one exponent of two for each 128 x 128 block.
All inputs are finite; a program needn't handle non-finite values.
Results may differ from a plain program's by a relative error of at most 0.035.
The roundings to bfloat16 on the way count: a program that leaves them out, or rounds other values in their place, can miss the bound.
Values may be sent and summed in bfloat16 or wider, within the bound.
A program may use at most 192 MiB of HBM per device.

v0:
```python
from functools import reduce
import math

import jax
import jax.numpy as jnp
from jax import lax
from jax.sharding import PartitionSpec as P

KV_HEADS = 4
Q_PER_KV = 8
HEAD = 128
BLOCK = 128
REACH = 4


theta_base = 500000.0
eps_norm = 1e-05
masked_score = -1e30


def passed_along(block, axis, distance):
    devices = range(lax.axis_size(axis))
    route = [(i - distance, i) for i in devices if i - distance in devices]
    return lax.ppermute(block, axis, route)


def rotary_tables(positions, head_size):
    half_size = head_size // 2
    frequency = theta_base ** (-(jnp.arange(half_size).astype(jnp.float32) * 2.0 / head_size))
    angles = positions.astype(jnp.float32)[:, None] * frequency[None, :]
    return (jnp.cos(angles)[:, None, :], jnp.sin(angles)[:, None, :])


def rotate(values, cosine, sine):
    half_size = values.shape[-1] // 2
    first = values[..., :half_size]
    second = values[..., half_size:]
    return jnp.concatenate(
        [first * cosine - second * sine, second * cosine + first * sine], axis=-1
    )


def unrotate(grads, cosine, sine):
    half_size = grads.shape[-1] // 2
    first = grads[..., :half_size]
    second = grads[..., half_size:]
    return jnp.concatenate(
        [first * cosine + second * sine, second * cosine - first * sine], axis=-1
    )


def doc_info(token_index, doc_lengths):
    starts = jnp.cumsum(doc_lengths) - doc_lengths
    before = starts[None, :] <= token_index[:, None]
    doc_number = jnp.sum(before.astype(jnp.int32), axis=1) - 1
    doc_start = jnp.max(jnp.where(before, starts[None, :], 0), axis=1)
    return (doc_number, token_index - doc_start)


def dequantize(values, exponents, block_side):
    row_blocks, col_blocks = exponents.shape
    factors = jnp.exp2(exponents.astype(jnp.float32))
    shaped = values.astype(jnp.float32).reshape(row_blocks, block_side, col_blocks, block_side)
    return (shaped * factors[:, None, :, None]).reshape(values.shape).astype(jnp.bfloat16)


def guarded(compute):
    result = compute()
    return result


def on_device(
    layer_input,
    queries,
    out_grad,
    top_grad,
    norm_gain,
    key_weight,
    value_weight,
    weight_exponents,
    doc_lengths,
):
    local_rows = layer_input.shape[1]
    kv_heads = KV_HEADS
    group_size = Q_PER_KV
    head_size = HEAD
    dp_index = lax.axis_index("dp")
    section_index = lax.axis_index("pipe")
    sections = lax.axis_size("pipe")
    key_local = dequantize(key_weight[0], weight_exponents[0, 0], BLOCK)
    value_local = dequantize(value_weight[0], weight_exponents[0, 1], BLOCK)
    key_full, value_full, gain_full = (
        lax.all_gather(key_local, "dp", axis=0, tiled=True),
        lax.all_gather(value_local, "dp", axis=0, tiled=True),
        lax.all_gather(norm_gain[0], "dp", axis=0, tiled=True),
    )
    inputs = layer_input[0].astype(jnp.float32)
    root_mean = jnp.sqrt(jnp.mean(inputs * inputs, axis=1, keepdims=True) + eps_norm)
    normed = inputs / root_mean
    gain_f = gain_full.astype(jnp.float32)
    hidden = (normed * gain_f).astype(jnp.bfloat16)
    token_index = dp_index * local_rows + jnp.arange(local_rows)
    query_doc, query_pos = doc_info(token_index, doc_lengths)
    cosine, sine = rotary_tables(query_pos, head_size)
    key_proj = jnp.dot(hidden, key_full, preferred_element_type=jnp.float32).reshape(
        local_rows, kv_heads, head_size
    )
    keys_own = rotate(key_proj, cosine, sine).astype(jnp.bfloat16)
    values_own = (
        jnp.dot(hidden, value_full, preferred_element_type=jnp.float32)
        .astype(jnp.bfloat16)
        .reshape(local_rows, kv_heads, head_size)
    )
    key_blocks = [None] * (REACH + 1)
    value_blocks = [None] * (REACH + 1)
    key_blocks[REACH] = keys_own
    value_blocks[REACH] = values_own
    own_pair = jnp.stack((keys_own, values_own))
    for distance in range(1, REACH + 1):
        got_pair = passed_along(own_pair, "dp", distance)
        key_blocks[REACH - distance] = got_pair[0]
        value_blocks[REACH - distance] = got_pair[1]
    inv_root = 1.0 / math.sqrt(head_size)
    query_groups = queries[0].reshape(local_rows, kv_heads, group_size, head_size)
    grad_groups = out_grad[0].reshape(local_rows, kv_heads, group_size, head_size)
    visibility = []
    seen_flags = []
    for block_number in range(REACH + 1):
        key_index = (dp_index - REACH + block_number) * local_rows + jnp.arange(local_rows)
        key_doc, unused = doc_info(key_index, doc_lengths)
        visible = (
            (key_index[None, :] >= 0)
            & (key_doc[None, :] == query_doc[:, None])
            & (key_index[None, :] <= token_index[:, None])
        )
        visibility.append(visible)
        seen_flags.append(jnp.any(visible))

    def score_block(block_number):

        def compute():
            raw_scores = jnp.einsum(
                "qkgd,tkd->kgqt",
                query_groups,
                key_blocks[block_number],
                preferred_element_type=jnp.float32,
            )
            return jnp.where(
                visibility[block_number][None, None], raw_scores * inv_root, masked_score
            )

        return guarded(compute)

    scores = [score_block(block_number) for block_number in range(REACH + 1)]
    row_max = reduce(jnp.maximum, [jnp.max(member, axis=3, keepdims=True) for member in scores])
    exp_scores = [jnp.exp(member - row_max) for member in scores]
    row_total = reduce(jnp.add, [jnp.sum(member, axis=3, keepdims=True) for member in exp_scores])
    softmax_out = [member / row_total for member in exp_scores]
    probs_low = [member.astype(jnp.bfloat16) for member in softmax_out]

    def attend_block(block_number):

        def compute():
            return jnp.einsum(
                "kgqt,tkd->qkgd",
                probs_low[block_number],
                value_blocks[block_number],
                preferred_element_type=jnp.float32,
            )

        return guarded(compute)

    attended = reduce(jnp.add, [attend_block(block_number) for block_number in range(REACH + 1)])
    out_dot = jnp.transpose(jnp.sum(grad_groups.astype(jnp.float32) * attended, axis=3), (1, 2, 0))[
        ..., None
    ]

    def grads_block(block_number):

        def compute():
            value_term = jnp.einsum(
                "kgqt,qkgd->tkd",
                probs_low[block_number],
                grad_groups,
                preferred_element_type=jnp.float32,
            )
            prob_grad = jnp.einsum(
                "qkgd,tkd->kgqt",
                grad_groups,
                value_blocks[block_number],
                preferred_element_type=jnp.float32,
            )
            score_grads = (softmax_out[block_number] * (prob_grad - out_dot)).astype(jnp.bfloat16)
            query_term = jnp.einsum(
                "kgqt,tkd->qkgd",
                score_grads,
                key_blocks[block_number],
                preferred_element_type=jnp.float32,
            )
            key_term = (
                jnp.einsum(
                    "kgqt,qkgd->tkd", score_grads, query_groups, preferred_element_type=jnp.float32
                )
                * inv_root
            )
            return (query_term, key_term.astype(jnp.bfloat16), value_term.astype(jnp.bfloat16))

        return guarded(compute)

    block_grads = [grads_block(block_number) for block_number in range(REACH + 1)]
    query_grad = (
        (reduce(jnp.add, [member[0] for member in block_grads]) * inv_root)
        .astype(jnp.bfloat16)
        .reshape(1, local_rows, -1)
    )
    key_sum = block_grads[REACH][1].astype(jnp.float32)
    value_sum = block_grads[REACH][2].astype(jnp.float32)
    for distance in range(1, REACH + 1):
        sent_pair = jnp.stack((block_grads[REACH - distance][1], block_grads[REACH - distance][2]))
        back_pair = passed_along(sent_pair, "dp", -distance)
        key_sum = key_sum + back_pair[0].astype(jnp.float32)
        value_sum = value_sum + back_pair[1].astype(jnp.float32)
    key_grads = unrotate(key_sum, cosine, sine).astype(jnp.bfloat16).reshape(local_rows, -1)
    value_grads = value_sum.astype(jnp.bfloat16).reshape(local_rows, -1)
    hidden_grad = jnp.einsum(
        "tc,dc->td", key_grads, key_full, preferred_element_type=jnp.float32
    ) + jnp.einsum("tc,dc->td", value_grads, value_full, preferred_element_type=jnp.float32)
    gain_term = jnp.sum(hidden_grad * normed, axis=0)
    scaled_grad = hidden_grad * gain_f
    branch = (
        scaled_grad - normed * jnp.mean(scaled_grad * normed, axis=1, keepdims=True)
    ) / root_mean
    last_section = sections - 1
    carried = jnp.where(
        section_index == last_section,
        (top_grad.astype(jnp.float32) + branch).astype(jnp.bfloat16),
        jnp.zeros_like(top_grad),
    )
    for step_number in range(sections - 1):
        received = passed_along(carried, "pipe", -1)
        carried = jnp.where(
            section_index == last_section - 1 - step_number,
            (received.astype(jnp.float32) + branch).astype(jnp.bfloat16),
            carried,
        )
    key_full_grad = jnp.einsum("tr,tc->rc", hidden, key_grads, preferred_element_type=jnp.float32)
    value_full_grad = jnp.einsum(
        "tr,tc->rc", hidden, value_grads, preferred_element_type=jnp.float32
    )
    key_wgrad, value_wgrad, gain_grad = (
        lax.psum_scatter(
            key_full_grad.astype(jnp.bfloat16), "dp", scatter_dimension=0, tiled=True
        ).astype(jnp.float32),
        lax.psum_scatter(
            value_full_grad.astype(jnp.bfloat16), "dp", scatter_dimension=0, tiled=True
        ).astype(jnp.float32),
        lax.psum_scatter(
            gain_term.astype(jnp.bfloat16), "dp", scatter_dimension=0, tiled=True
        ).astype(jnp.float32),
    )
    return (carried[None], query_grad, key_wgrad[None], value_wgrad[None], gain_grad[None])


def solution(mesh):
    in_specs = (
        P("pipe", "dp", None),
        P("pipe", "dp", None),
        P("pipe", "dp", None),
        P("dp", None),
        P("pipe", "dp"),
        P("pipe", "dp", None),
        P("pipe", "dp", None),
        P("pipe", None, "dp", None),
        P(),
    )
    out_specs = (
        P("pipe", "dp", None),
        P("pipe", "dp", None),
        P("pipe", "dp", None),
        P("pipe", "dp", None),
        P("pipe", "dp"),
    )
    return jax.shard_map(
        on_device, mesh=mesh, in_specs=in_specs, out_specs=out_specs, check_vma=False
    )
```

profile of v0, /device:TPU:0, one launch (start us, length us, event | category | flops | bytes accessed | tf_op | source)
XLA Modules:
  0.0 964.3 jit_solution(9609781831915114517)
XLA Ops:
  8.2 1.7 fusion.70
  11.0 82.9 %all-gather = bf16[1,8192]{1,0:T(2,128)(2,1)S(1)} all-gather(bf16[1,256]{1,0:T(2,128)(2,1)S(1)} %copy-done.38), channel_id=2, replica_groups=mesh['pipe'=4,'dp'=32] {'dp'}, dimensions={1}, use_global_device_ids=true | all-gather | bytes 16896 | tf_op jit(solution)/shard_map/all_gather | solution.py:95
  95.5 2.1 fusion.2
  97.9 0.9 compare_and_fusion.3
  98.8 104.8 %all-gather.6.cloned.1.call-done = bf16[8192,512]{1,0:T(8,128)(2,1)} async-done(((bf16[256,512]{1,0:T(8,128)(2,1)}), bf16[8192,512]{1,0:T(8,128)(2,1)}) %all-gather.6.cloned.1.call-update) | async-done | bytes 8388624 | tf_op jit(solution)/shard_map/all_gather | solution.py:94
  203.7 5.3 fusion.49
  209.1 184.8 %all-gather.4.cloned.1.call-done = bf16[8192,512]{1,0:T(8,128)(2,1)} async-done(((bf16[256,512]{1,0:T(8,128)(2,1)}), bf16[8192,512]{1,0:T(8,128)(2,1)}) %all-gather.4.cloned.1.call-update) | async-done | bytes 8388624 | tf_op jit(solution)/shard_map/all_gather | solution.py:93
  393.9 12.0 %copy.180 = bf16[512,8192]{1,0:T(8,128)(2,1)} copy(bf16[512,8192]{0,1:T(8,128)(2,1)} %bitcast.450) | data formatting | bytes 16777216 | tf_op jit(solution)/shard_map/dot_general | solution.py:105
  406.0 6.4 fusion.22
  413.2 1.3 collective-permute-start.3
  414.5 1.5 collective-permute-start.2
  416.0 4.1 collective-permute-start.1
  420.1 5.6 collective-permute-start
  425.9 1.4 fusion.100
  427.3 8.9 collective-permute-done
  439.0 3.3 fusion.32
  442.3 2.1 fusion.65
  447.9 1.0 fusion.19
  455.1 1.4 collective-permute-start.4
  456.6 1.3 collective-permute-start.5
  457.9 1.3 collective-permute-start.6
  459.3 1.5 collective-permute-start.7
  460.8 4.6 collective-permute-done.4
  465.4 7.0 collective-permute-done.5
  472.3 1.1 collective-permute-done.7
  474.8 5.7 convolution_convert_fusion
  480.6 2.4 fusion.21
  484.1 1.0 copy-done.2
  485.1 5.7 convolution_convert_fusion.1
  490.9 6.4 fusion.106
  497.3 6.0 multiply_reduce_fusion
  503.4 2.8 fusion.6
  506.1 1.3 collective-permute-start.8
  507.4 4.9 collective-permute-done.8
  512.3 4.9 fusion.7
  517.2 1.5 collective-permute-start.9
  518.8 71.2 %collective-permute-done.9 = bf16[128,8192]{1,0:T(8,128)(2,1)} collective-permute-done((bf16[128,8192]{1,0:T(8,128)(2,1)}, bf16[128,8192]{1,0:T(8,128)(2,1)}, u32[]{:S(2)}, u32[]{:S(2)}) %collective-permute-start.9) | collective-permute-done | bytes 2097184 | tf_op jit(solution)/shard_map/ppermute | solution.py:24
  589.9 6.0 fusion.8
  595.9 1.3 collective-permute-start.10
  597.2 1.2 dynamic-slice
  599.1 1.7 fusion.81
  603.5 0.8 copy-done.13
  605.1 1.3 copy.233
  606.4 171.9 %all-reduce = bf16[8192]{0:T(1024)(128)(2,1)S(1)} all-reduce(bf16[8192]{0:T(1024)(128)(2,1)S(1)} %get-tuple-element.25), channel_id=5, replica_groups=mesh['pipe'=4,'dp'=32] {'dp'}, use_global_device_ids=true, to_apply=%region_23.24.clone | all-reduce | flops 8192 | bytes 32768
  778.9 7.0 fusion.10
  786.0 1.8 bitcast_convert_fusion
  787.8 167.9 %reduce-scatter.3.cloned.1.call-done = bf16[256,512]{1,0:T(8,128)(2,1)} async-done(((bf16[8192,512]{1,0:T(8,128)(2,1)}), bf16[256,512]{1,0:T(8,128)(2,1)}) %reduce-scatter.3.cloned.1.call-update) | async-done | bytes 262160 | tf_op jit(solution)/shard_map/reduce_scatter | solution.py:251
  955.7 1.8 bitcast_convert_fusion.1
  (187 shorter events, 23.5 us)
Async XLA Ops:
  7.2 3.0 copy-start.28
  7.2 3.9 copy-start.38
  7.2 86.8 %copy-start.43 = (s32[64]{0:T(128)S(1)}, s32[64]{0:T(128)}, u32[]{:S(2)}) copy-start(s32[64]{0:T(128)} %param.17) | copy-start | bytes 772
  7.2 87.1 %copy-start.10 = (bf16[1,128,4096]{2,1,0:T(8,128)(2,1)S(1)}, bf16[1,128,4096]{2,1,0:T(8,128)(2,1)}, u32[]{:S(2)}) copy-start(bf16[1,128,4096]{2,1,0:T(8,128)(2,1)} %param.10) | copy-start | bytes 3145732
  7.2 196.4 %all-gather.6.cloned.1.call-start = ((), (), s32[]{:S(2)}) async-start(), calls=%async_computation.3 | async-start | bytes 8650752 | tf_op jit(solution)/shard_map/all_gather | solution.py:94
  9.9 384.0 %all-gather.4.cloned.1.call-start = ((), (), s32[]{:S(2)}) async-start(), calls=%async_computation.2 | async-start | bytes 8650752 | tf_op jit(solution)/shard_map/all_gather | solution.py:93
  10.0 84.6 %copy-start.11 = (bf16[1,128,4096]{2,1,0:T(8,128)(2,1)S(1)}, bf16[1,128,4096]{2,1,0:T(8,128)(2,1)}, u32[]{:S(2)}) copy-start(bf16[1,128,4096]{2,1,0:T(8,128)(2,1)} %param.11) | copy-start | bytes 3145732
  11.0 775.0 %reduce-scatter.5.cloned.1.call-start = ((), (), s32[]{:S(2)}) async-start(), calls=%async_computation.5 | async-start | bytes 8650752 | tf_op jit(solution)/shard_map/reduce_scatter | solution.py:254
  94.0 312.0 %copy-start.29 = (f32[1,8192]{1,0:T(1,128)}, f32[1,8192]{1,0:T(1,128)S(1)}, u32[]{:S(2)}) copy-start(f32[1,8192]{1,0:T(1,128)S(1)} %convert_element_type.409) | copy-start | bytes 98308
  97.6 308.4 %copy-start.39 = (f32[128]{0:T(128)}, f32[128]{0:T(128)S(1)}, u32[]{:S(2)}) copy-start(f32[128]{0:T(128)S(1)} %add_sqrt_fusion) | copy-start | bytes 1540
  97.9 314.5 %copy-start.24 = (f32[128,64]{0,1:T(8,128)}, f32[128,64]{0,1:T(8,128)S(1)}, u32[]{:S(2)}) copy-start(f32[128,64]{0,1:T(8,128)S(1)} %get-tuple-element.56) | copy-start | bytes 98308
  97.9 314.5 %copy-start.26 = (f32[128,64]{0,1:T(8,128)}, f32[128,64]{0,1:T(8,128)S(1)}, u32[]{:S(2)}) copy-start(f32[128,64]{0,1:T(8,128)S(1)} %get-tuple-element.57) | copy-start | bytes 98308
  413.2 25.1 %collective-permute-start.3 = (bf16[2,128,4,128]{1,3,2,0:T(8,128)(2,1)}, bf16[2,128,4,128]{1,3,2,0:T(8,128)(2,1)S(1)}, u32[]{:S(2)}, u32[]{:S(2)}) collective-permute-start(bf16[2,128,4,128]{1,3,2,0:T(8,128)(2,1)} %pad_maximum_fusion), channel_id=1, source_target_pairs={{0,1},{1,2},{2,3},{3,4},{4,5},{5,6},{6,7},{7,8},{8,9},{9,10},{10,1... | collective-permute-start | bytes 786440 | tf_op jit(solution)/shard_map/ppermute | solution.py:24
  414.5 23.1 %collective-permute-start.2 = (bf16[2,128,4,128]{1,3,2,0:T(8,128)(2,1)}, bf16[2,128,4,128]{1,3,2,0:T(8,128)(2,1)S(1)}, u32[]{:S(2)}, u32[]{:S(2)}) collective-permute-start(bf16[2,128,4,128]{1,3,2,0:T(8,128)(2,1)} %pad_maximum_fusion), channel_id=1, source_target_pairs={{0,2},{1,3},{2,4},{3,5},{4,6},{5,7},{6,8},{7,9},{8,10},{9,11},{10,... | collective-permute-start | bytes 786440 | tf_op jit(solution)/shard_map/ppermute | solution.py:24
  416.0 20.9 %collective-permute-start.1 = (bf16[2,128,4,128]{1,3,2,0:T(8,128)(2,1)}, bf16[2,128,4,128]{1,3,2,0:T(8,128)(2,1)S(1)}, u32[]{:S(2)}, u32[]{:S(2)}) collective-permute-start(bf16[2,128,4,128]{1,3,2,0:T(8,128)(2,1)} %pad_maximum_fusion), channel_id=1, source_target_pairs={{0,3},{1,4},{2,5},{3,6},{4,7},{5,8},{6,9},{7,10},{8,11},{9,12},{10... | collective-permute-start | bytes 786440 | tf_op jit(solution)/shard_map/ppermute | solution.py:24
  420.1 16.1 %collective-permute-start = (bf16[2,128,4,128]{1,3,2,0:T(8,128)(2,1)}, bf16[2,128,4,128]{1,3,2,0:T(8,128)(2,1)S(1)}, u32[]{:S(2)}, u32[]{:S(2)}) collective-permute-start(bf16[2,128,4,128]{1,3,2,0:T(8,128)(2,1)} %pad_maximum_fusion), channel_id=1, source_target_pairs={{0,4},{1,5},{2,6},{3,7},{4,8},{5,9},{6,10},{7,11},{8,12},{9,13},{1... | collective-permute-start | bytes 786440 | tf_op jit(solution)/shard_map/ppermute | solution.py:24
  425.8 20.3 %copy-start.23 = (bf16[128,4,128,1]{0,2,3,1:T(8,128)(2,1)}, bf16[128,4,128,1]{0,2,3,1:T(8,128)(2,1)S(1)}, u32[]{:S(2)}) copy-start(bf16[128,4,128,1]{0,2,3,1:T(8,128)(2,1)S(1)} %copy.249) | copy-start | bytes 393220
  425.9 10.3 %copy-start.35 = (pred[128,128]{0,1:T(8,128)(4,1)S(1)}, pred[128,128]{0,1:T(8,128)(4,1)}, u32[]{:S(2)}) copy-start(pred[128,128]{0,1:T(8,128)(4,1)} %get-tuple-element.51) | copy-start | bytes 49156
  427.3 15.0 %copy-start = (f32[4,8,128,128]{2,3,1,0:T(8,128)}, f32[4,8,128,128]{2,3,1,0:T(8,128)S(1)}, u32[]{:S(2)}) copy-start(f32[4,8,128,128]{2,3,1,0:T(8,128)S(1)} %get-tuple-element.59) | copy-start | bytes 6291460
  427.3 9.6 copy-start.34
  436.2 11.2 %copy-start.17 = (bf16[2,128,4,128]{1,3,2,0:T(8,128)(2,1)}, bf16[2,128,4,128]{1,3,2,0:T(8,128)(2,1)S(1)}, u32[]{:S(2)}) copy-start(bf16[2,128,4,128]{1,3,2,0:T(8,128)(2,1)S(1)} %collective-permute-done) | copy-start | bytes 786436
  436.9 10.1 %copy-start.14 = (bf16[2,128,4,128]{1,3,2,0:T(8,128)(2,1)}, bf16[2,128,4,128]{1,3,2,0:T(8,128)(2,1)S(1)}, u32[]{:S(2)}) copy-start(bf16[2,128,4,128]{1,3,2,0:T(8,128)(2,1)S(1)} %collective-permute-done.1) | copy-start | bytes 786436
  438.3 9.6 copy-start.20
  442.3 10.9 %copy-start.36 = (f32[4,8,128]{2,1,0:T(8,128)}, f32[4,8,128]{2,1,0:T(8,128)S(1)}, u32[]{:S(2)}) copy-start(f32[4,8,128]{2,1,0:T(8,128)S(1)} %add_add_fusion) | copy-start | bytes 49156
  448.9 4.4 copy-start.37
  454.4 4.9 copy-start.12
  455.1 19.7 %copy-start.1 = (bf16[1,128,8192]{2,1,0:T(8,128)(2,1)S(1)}, bf16[1,128,8192]{2,1,0:T(8,128)(2,1)}, u32[]{:S(2)}) copy-start(bf16[1,128,8192]{2,1,0:T(8,128)(2,1)} %param.9) | copy-start | bytes 6291460
  455.1 19.7 %copy-start.30 = (f32[1,8192]{1,0:T(1,128)S(1)}, f32[1,8192]{1,0:T(1,128)}, u32[]{:S(2)}) copy-start(f32[1,8192]{1,0:T(1,128)} %copy-done.29) | copy-start | bytes 98308
  455.1 19.7 %copy-start.40 = (f32[128]{0:T(128)S(1)}, f32[128]{0:T(128)}, u32[]{:S(2)}) copy-start(f32[128]{0:T(128)} %copy-done.39) | copy-start | bytes 1540
  455.1 10.3 %collective-permute-start.4 = (bf16[2,128,4,128]{1,3,2,0:T(8,128)(2,1)S(1)}, bf16[2,128,4,128]{1,3,2,0:T(8,128)(2,1)S(1)}, u32[]{:S(2)}, u32[]{:S(2)}) collective-permute-start(bf16[2,128,4,128]{1,3,2,0:T(8,128)(2,1)S(1)} %pad_maximum_fusion.1), channel_id=1, source_target_pairs={{1,0},{2,1},{3,2},{4,3},{5,4},{6,5},{7,6},{8,7},{9,8},{10,9},{11,1... | collective-permute-start | bytes 786440 | tf_op jit(solution)/shard_map/ppermute | solution.py:24
  456.6 15.7 %collective-permute-start.5 = (bf16[2,128,4,128]{1,3,2,0:T(8,128)(2,1)S(1)}, bf16[2,128,4,128]{1,3,2,0:T(8,128)(2,1)S(1)}, u32[]{:S(2)}, u32[]{:S(2)}) collective-permute-start(bf16[2,128,4,128]{1,3,2,0:T(8,128)(2,1)S(1)} %pad_maximum_fusion.2), channel_id=1, source_target_pairs={{2,0},{3,1},{4,2},{5,3},{6,4},{7,5},{8,6},{9,7},{10,8},{11,9},{12,... | collective-permute-start | bytes 786440 | tf_op jit(solution)/shard_map/ppermute | solution.py:24
  457.9 14.4 %collective-permute-start.6 = (bf16[2,128,4,128]{1,3,2,0:T(8,128)(2,1)S(1)}, bf16[2,128,4,128]{1,3,2,0:T(8,128)(2,1)S(1)}, u32[]{:S(2)}, u32[]{:S(2)}) collective-permute-start(bf16[2,128,4,128]{1,3,2,0:T(8,128)(2,1)S(1)} %pad_maximum_fusion.3), channel_id=1, source_target_pairs={{3,0},{4,1},{5,2},{6,3},{7,4},{8,5},{9,6},{10,7},{11,8},{12,9},{13... | collective-permute-start | bytes 786440 | tf_op jit(solution)/shard_map/ppermute | solution.py:24
  459.3 14.2 %collective-permute-start.7 = (bf16[2,128,4,128]{1,3,2,0:T(8,128)(2,1)S(1)}, bf16[2,128,4,128]{1,3,2,0:T(8,128)(2,1)S(1)}, u32[]{:S(2)}, u32[]{:S(2)}) collective-permute-start(bf16[2,128,4,128]{1,3,2,0:T(8,128)(2,1)S(1)} %pad_maximum_fusion.4), channel_id=1, source_target_pairs={{4,0},{5,1},{6,2},{7,3},{8,4},{9,5},{10,6},{11,7},{12,8},{13,9},{1... | collective-permute-start | bytes 786440 | tf_op jit(solution)/shard_map/ppermute | solution.py:24
  465.4 8.5 copy-start.44
  480.5 475.2 %reduce-scatter.3.cloned.1.call-start = ((), (), s32[]{:S(2)}) async-start(), calls=%async_computation.4 | async-start | bytes 8650752 | tf_op jit(solution)/shard_map/reduce_scatter | solution.py:251
  480.6 2.5 copy-start.45
  480.6 2.5 copy-start.47
  480.6 2.5 copy-start.49
  480.6 2.5 copy-start.51
  483.1 2.0 copy-start.2
  490.8 6.4 copy-start.3
  490.9 6.4 copy-start.53
  497.3 6.1 copy-start.4
  497.3 6.1 copy-start.32
  497.3 6.1 copy-start.42
  506.1 6.2 collective-permute-start.8
  517.2 72.7 %collective-permute-start.9 = (bf16[128,8192]{1,0:T(8,128)(2,1)}, bf16[128,8192]{1,0:T(8,128)(2,1)}, u32[]{:S(2)}, u32[]{:S(2)}) collective-permute-start(bf16[128,8192]{1,0:T(8,128)(2,1)} %fusion.7), channel_id=1, source_target_pairs={{32,0},{64,32},{96,64},{33,1},{65,33},{97,65},{34,2},{66,34},{98,6... | collective-permute-start | bytes 6291464 | tf_op jit(solution)/shard_map/ppermute | solution.py:24
  595.9 183.0 %collective-permute-start.10 = (bf16[128,8192]{1,0:T(8,128)(2,1)}, bf16[128,8192]{1,0:T(8,128)(2,1)}, u32[]{:S(2)}, u32[]{:S(2)}) collective-permute-start(bf16[128,8192]{1,0:T(8,128)(2,1)} %fusion.8), channel_id=1, source_target_pairs={{32,0},{64,32},{96,64},{33,1},{65,33},{97,65},{34,2},{66,34},{98,6... | collective-permute-start | bytes 6291464 | tf_op jit(solution)/shard_map/ppermute | solution.py:24
  (21 other events, 26.0 us)
Sparse Core Ops, SparseCore 0:
  10.3 193.3 all-gather.5
  205.9 187.9 all-gather.3
  480.6 214.8 reduce-scatter.4
  697.9 257.8 reduce-scatter.2
where the time goes:
time: 971 us; the launch traced here: 964 us
  waiting for transfers between devices  555 us (57%)
  blocking collectives  255 us (26%)
  matrix products  56.6 us (6%)
  other arithmetic  38.2 us (4%)
  starting transfers between devices  22.3 us (2%)
  local copies, waits for them, and re-layouts  21.4 us (2%)
  between operations  15.9 us (2%)
    all_gather x1, waiting for transfers between devices, on_device(): lax.all_gather(key_local, 'dp', axis=0, tiled=True)  185 us
    unnamed x1, blocking collectives  172 us
    reduce_scatter x1, waiting for transfers between devices, on_device(): lax.psum_scatter(key_full_grad.astype(jnp.bfloat16), 'dp', scatter_dimens...  168 us
    all_gather x1, waiting for transfers between devices, on_device(): lax.all_gather(value_local, 'dp', axis=0, tiled=True)  105 us
    ppermute x11, waiting for transfers between devices, passed_along(): return lax.ppermute(block, axis, route)  97.5 us
    all_gather x1, blocking collectives, on_device(): lax.all_gather(norm_gain[0], 'dp', axis=0, tiled=True)  82.9 us
    ppermute x11, starting transfers between devices, passed_along(): return lax.ppermute(block, axis, route)  22.1 us
  transfers between devices with their start and end apart: 15, of which 9 were waited for; matrix products, arithmetic and copies ran while one was open for 7% of the time, Pallas kernels for 0%

commit v1 on v0

v1 whole, which is shorter than its diff:
```python
import functools
import math

import jax
import jax.numpy as jnp
import numpy as np
from jax import lax
from jax.experimental import pallas as pl
from jax.experimental.pallas import tpu as pltpu
from jax.sharding import PartitionSpec as P

D = 8192
KV_HEADS = 4
Q_PER_KV = 8
HEAD = 128
TOK = 128
REACH = 4
KVW = 512
QW = 4096
ROWS = 256
THETA = 500000.0
EPS = 1e-05
MASKED = -1e30

F = 8
T = 4
SLAB = 1024
WIN = (REACH + 1) * TOK
CHUNKS = 8
PAIR = 2

MESH = pl.DeviceIdType.MESH
NT = (((1,), (1,)), ((), ()))
NN = (((1,), (0,)), ((), ()))


def rows(start, size):
    return pl.ds(pl.multiple_of(start, size), size)


def cols(start, size):
    return pl.ds(pl.multiple_of(start, size), size)


def dot(a, b, dims=NN):
    return lax.dot_general(a, b, dims, preferred_element_type=jnp.float32)


def wide(col, width):
    return jnp.concatenate([col] * (width // col.shape[1]), axis=1)


def kernel(
    fac, docs, freq, x, q, do, top, gain, kw, vw,
    o_in, o_q, o_kw, o_vw, o_gain,
    xs, xr, kwv, vwv, wr, gr, rr, rown, qs, dos, cin, cout, cosb, sinb, bias,
    hbuf, ht, psend, precv, kwin, pt, dst, tb, ra, dq, gall, hgs, sgr, ab, bb,
    ws, wrecv, wown, gs, grecv, gacc,
    lsem, sx, rx, sr, rrs, sw, rw, sg, rg, sp, rp, skv, rkv, sb, rb,
    sga, rga, sh, rh, sws, rws, sgs, rgs, src_, rrc, osem,
):
    p = lax.axis_index("pipe")
    i = lax.axis_index("dp")
    f = i % F
    t = i // F
    xl = i % 2

    def slab(k, size=TOK):
        return slice(k * size, (k + 1) * size)

    def f_up(k):
        return (p, t * F + (f + k) % F)

    def f_down(k):
        return (p, t * F + (f + F - k) % F)

    def t_up(k):
        return (p, (t + k) % T * F + f)

    def t_down(k):
        return (p, (t + T - k) % T * F + f)

    def rcopy(src, dst, ssem, rsem, dev):
        return pltpu.make_async_remote_copy(
            src_ref=src, dst_ref=dst, send_sem=ssem, recv_sem=rsem,
            device_id=dev, device_id_type=MESH)

    def x_cols(n):
        return cols(((t + T - n % T) % T * F + (f + n // T) % F) * ROWS, ROWS)

    def load_x(n, carry):
        pltpu.make_async_copy(x.at[0, :, x_cols(n)], xs.at[n], lsem.at[0]).start()
        return carry

    lax.fori_loop(0, F * T, load_x, 0)
    pltpu.make_async_copy(kw.at[0], kwv, lsem.at[1]).start()
    pltpu.make_async_copy(vw.at[0], vwv, lsem.at[2]).start()

    def load_q(n, carry):
        pltpu.make_async_copy(
            q.at[0, :, cols(n * HEAD, HEAD)], qs.at[rows(n * TOK, TOK)], lsem.at[3]).start()
        pltpu.make_async_copy(
            do.at[0, :, cols(n * HEAD, HEAD)], dos.at[rows(n * TOK, TOK)], lsem.at[4]).start()
        return carry

    lax.fori_loop(0, KV_HEADS * Q_PER_KV, load_q, 0)

    @pl.when(p == 3)
    def _():
        def load_top(n, carry):
            pltpu.make_async_copy(top.at[:, x_cols(n)], cin.at[n], lsem.at[5]).start()
            return carry

        lax.fori_loop(0, F * T, load_top, 0)

    barrier = pltpu.get_barrier_semaphore()
    peers = [f_up(k) for k in range(1, F)] + [t_up(k) for k in range(1, T)]
    peers += [(p, (i + 2) % 32), (p, (i + 30) % 32)]
    peers += [((p + 1) % 4, i), ((p + 3) % 4, i)]
    for peer in peers:
        pl.semaphore_signal(barrier, inc=1, device_id=peer, device_id_type=MESH)
    pl.semaphore_wait(barrier, len(peers))

    pltpu.make_async_copy(xs, xs, lsem.at[0]).wait()

    def x_copy(k):
        return rcopy(xs.at[slab(k, T)], xr.at[slab(k, T)], sx.at[k], rx.at[k], f_up(k))

    for k in range(1, F):
        x_copy(k).start()
    xr[0:T] = xs[0:T]

    pltpu.make_async_copy(kw.at[0], kwv, lsem.at[1]).wait()
    pltpu.make_async_copy(vw.at[0], vwv, lsem.at[2]).wait()
    for rblock in range(2):
        for cblock in range(4):
            for which, wv in ((0, kwv), (1, vwv)):
                block = wv[slab(rblock), slab(cblock)].astype(jnp.float32)
                scaled = block * fac[which * 8 + rblock * 4 + cblock]
                wr[slab(rblock), slab(which * 4 + cblock)] = scaled.astype(jnp.bfloat16)
    gr[0:8, :] = jnp.broadcast_to(gain[...].astype(jnp.float32), (8, ROWS))

    def w_copy(k):
        return rcopy(wr.at[0:ROWS], wr.at[slab(k, ROWS)], sw.at[k], rw.at[k], t_up(k))

    def g_copy(k):
        return rcopy(gr.at[0:8], gr.at[slab(k, 8)], sg.at[k], rg.at[k], t_up(k))

    for k in range(1, T):
        w_copy(k).start()
        g_copy(k).start()

    def add_squares(n, acc):
        part = xs[n].astype(jnp.float32)
        part = part * part
        for c in range(ROWS // 128):
            acc = acc + part[:, slab(c)]
        return acc

    squares = lax.fori_loop(0, F * T, add_squares, jnp.zeros((TOK, 128), jnp.float32))
    mean_sq = jnp.sum(squares, axis=1, keepdims=True) * (1.0 / D)
    rinv = jnp.broadcast_to(1.0 / jnp.sqrt(mean_sq + EPS), (TOK, 128))
    rown[...] = rinv
    rr[0:8, :] = rinv.T[0:8, :]

    def r_copy(k):
        return rcopy(rr.at[0:8], rr.at[slab(k, 8)], sr.at[k], rrs.at[k], f_up(k))

    for k in range(1, F):
        r_copy(k).start()

    tok_col = i * TOK + lax.broadcasted_iota(jnp.int32, (TOK, 128), 0)
    tok_row = i * TOK + lax.broadcasted_iota(jnp.int32, (8, 128), 1)

    def scan_docs(n, carry):
        start, scol, srow = carry
        scol = jnp.where(start <= tok_col, start, scol)
        srow = jnp.where(start <= tok_row, start, srow)
        return start + docs[n], scol, srow

    _, scol, srow = lax.fori_loop(
        0, 64, scan_docs,
        (jnp.int32(0), jnp.zeros((TOK, 128), jnp.int32), jnp.zeros((8, 128), jnp.int32)))
    angle = (tok_col - scol).astype(jnp.float32) * freq[0:1, :]
    lane = lax.broadcasted_iota(jnp.int32, (TOK, 128), 1)
    sine = jnp.sin(angle)
    cosb[...] = jnp.cos(angle)
    sinb[...] = jnp.where(lane < 64, -sine, sine)
    key_index = (i - REACH) * TOK + lax.broadcasted_iota(jnp.int32, (WIN, 128), 0)
    seen = (key_index >= srow[0:1, :]) & (key_index <= tok_row[0:1, :])
    bias[...] = jnp.where(seen, 0.0, MASKED)

    for k in range(1, T):
        w_copy(k).wait_recv()
        g_copy(k).wait_recv()

    def inv_rms(k):
        return jnp.broadcast_to(rr[k * 8:k * 8 + 1, :], (TOK, 128)).T

    def slab_x(k):
        return jnp.concatenate(
            [xr[k * T + n].astype(jnp.float32) for n in range(T)], axis=1)

    gain_row = jnp.concatenate([gr[n * 8:n * 8 + 1, :] for n in range(T)], axis=1)

    def p_copy(k):
        return rcopy(psend.at[slab(k)], precv.at[slab(k)], sp.at[k], rp.at[k], f_down(k))

    for k in range(F):
        if k > 0:
            x_copy(k).wait_recv()
            r_copy(k).wait_recv()
        hidden = (slab_x(k) * wide(inv_rms(k), SLAB) * gain_row).astype(jnp.bfloat16)
        hbuf[slab(k), :] = hidden
        part = dot(hidden, wr[...]).astype(jnp.bfloat16)
        if k > 0:
            psend[slab(k), :] = part
            p_copy(k).start()
        else:
            precv[slab(k), :] = part

    for k in range(F):
        ht[:, slab(k)] = hbuf[slab(k), :].T

    for k in range(1, F):
        p_copy(k).wait_recv()

    def rope(block, sign):
        return block * cosb[...] + pltpu.roll(block, 64, 1) * (sinb[...] * sign)

    for c in range(8):
        total = precv[0:TOK, slab(c)].astype(jnp.float32)
        for k in range(1, F):
            total = total + precv[slab(k), slab(c)].astype(jnp.float32)
        if c < 4:
            total = rope(total, 1.0)
        kwin[REACH * TOK:, slab(c)] = total.astype(jnp.bfloat16)

    partner = (p, i + 1 - 2 * xl)
    ahead = (p, (i + 2) % 32)
    back = (p, (i + 30) % 32)

    def kv_copy(src, dst_slot, n, dev):
        return rcopy(kwin.at[slab(src)], kwin.at[slab(dst_slot)], skv.at[n], rkv.at[n], dev)

    hop1 = kv_copy(4, 2, 0, ahead)
    hop2 = kv_copy(2, 0, 1, ahead)
    even1 = kv_copy(4, 3, 2, partner)
    even2 = kv_copy(2, 1, 3, partner)
    odd1 = kv_copy(2, 3, 2, partner)
    odd2 = kv_copy(0, 1, 3, partner)
    hop1.start()

    @pl.when(xl == 0)
    def _():
        even1.start()

    hop1.wait_recv()
    hop2.start()

    @pl.when(xl == 0)
    def _():
        even2.start()

    @pl.when(xl == 1)
    def _():
        odd1.start()

    hop2.wait_recv()

    @pl.when(xl == 1)
    def _():
        odd2.start()

    pltpu.make_async_copy(qs, qs, lsem.at[3]).wait()
    pltpu.make_async_copy(dos, dos, lsem.at[4]).wait()
    even1.wait_recv()
    even2.wait_recv()

    inv_root = 1.0 / math.sqrt(HEAD)

    def one_kv_head(h, carry):
        kcol = cols(h * HEAD, HEAD)
        vcol = cols(KVW + h * HEAD, HEAD)
        keys = kwin[:, kcol]
        vals = kwin[:, vcol]
        keys_t = keys.T

        def heads(g, carry2):
            width = PAIR * TOK
            qrow = rows((h * Q_PER_KV + g * PAIR) * TOK, width)
            scores = dot(keys, qs[qrow, :], NT) * inv_root + wide(bias[...], width)
            top_score = jnp.max(scores, axis=0, keepdims=True)
            expd = jnp.exp(scores - top_score)
            probs = expd * (1.0 / jnp.sum(expd, axis=0, keepdims=True))
            low = probs.astype(jnp.bfloat16)
            pgrad = dot(vals, dos[qrow, :], NT)
            delta = jnp.sum(low.astype(jnp.float32) * pgrad, axis=0, keepdims=True)
            sgrad = (probs * (pgrad - delta)).astype(jnp.bfloat16)
            pcol = cols(g * width, width)
            pt[:, pcol] = low
            dst[:, pcol] = sgrad
            dqt = dot(keys_t, sgrad) * inv_root
            for n in range(PAIR):
                head = (h * Q_PER_KV + g * PAIR + n) * HEAD
                dq[:, cols(head, HEAD)] = dqt[:, slab(n)].T.astype(jnp.bfloat16)
            return carry2

        lax.fori_loop(0, Q_PER_KV // PAIR, heads, 0)
        hrow = rows(h * Q_PER_KV * TOK, Q_PER_KV * TOK)
        tb[:, vcol] = dot(pt[...], dos[hrow, :]).astype(jnp.bfloat16)
        tb[:, kcol] = (dot(dst[...], qs[hrow, :]) * inv_root).astype(jnp.bfloat16)
        return carry

    lax.fori_loop(0, KV_HEADS, one_kv_head, 0)

    def t_copy(src, n, dev):
        return rcopy(tb.at[slab(src)], ra.at[slab(n)], sb.at[n], rb.at[n], dev)

    back_a = t_copy(3, 0, partner)
    back_b = t_copy(1, 1, partner)
    back_c = t_copy(0, 2, back)
    back_d = t_copy(2, 3, back)
    back_b.start()
    back_a.start()

    def fold(s, n):
        tb[slab(s), :] = (tb[slab(s), :].astype(jnp.float32)
                          + ra[slab(n), :].astype(jnp.float32)).astype(jnp.bfloat16)

    back_b.wait_recv()

    @pl.when(xl == 1)
    def _():
        fold(0, 1)

    back_c.start()
    back_a.wait_recv()

    @pl.when(xl == 1)
    def _():
        fold(2, 0)

    @pl.when(xl == 0)
    def _():
        fold(2, 1)
        fold(4, 0)

    back_c.wait_recv()
    fold(2, 2)
    back_d.start()
    out_q = pltpu.make_async_copy(dq, o_q.at[0], osem.at[0])
    out_q.start()
    back_d.wait_recv()
    for c in range(8):
        total = (tb[slab(REACH), slab(c)].astype(jnp.float32)
                 + ra[slab(3), slab(c)].astype(jnp.float32))
        if c < 4:
            total = rope(total, -1.0)
        gall[0:TOK, slab(c)] = total.astype(jnp.bfloat16)

    def ga_copy(k):
        return rcopy(gall.at[0:TOK], gall.at[slab(k)], sga.at[k], rga.at[k], f_up(k))

    for k in range(1, F):
        ga_copy(k).start()

    gacc[...] = jnp.zeros_like(gacc)

    def h_copy(k):
        return rcopy(hgs.at[slab(k)], sgr.at[slab(k)], sh.at[k], rh.at[k], f_down(k))

    for k in range(F):
        if k > 0:
            ga_copy(k).wait_recv()
        hg = dot(gall[slab(k), :], wr[...], NT)
        scaled = (hg * gain_row).astype(jnp.bfloat16)
        if k > 0:
            hgs[slab(k), :] = scaled
            h_copy(k).start()
        else:
            sgr[slab(k), :] = scaled
        prod = hg * slab_x(k) * wide(inv_rms(k), SLAB)
        part = prod[0:8, :]
        for n in range(1, TOK // 8):
            part = part + prod[slab(n, 8), :]
        gacc[...] = gacc[...] + part

    gterm = jnp.broadcast_to(jnp.sum(gacc[...], axis=0, keepdims=True), (8, SLAB))
    for k in range(T):
        gs[slab(k, 8), :] = gterm[:, slab(k, ROWS)]

    def gs_copy(k):
        return rcopy(gs.at[slab(k, 8)], grecv.at[slab(k, 8)], sgs.at[k], rgs.at[k], t_down(k))

    def ws_copy(k):
        return rcopy(ws.at[slab(k, ROWS)], wrecv.at[slab(k, ROWS)], sws.at[k], rws.at[k],
                     t_down(k))

    for k in range(1, T):
        ws[slab(k, ROWS), :] = dot(ht[slab(k, ROWS), :], gall[...]).astype(jnp.bfloat16)
        ws_copy(k).start()
        gs_copy(k).start()
    wown[...] = dot(ht[0:ROWS, :], gall[...])

    dots = jnp.zeros((TOK, 128), jnp.float32)
    for k in range(F):
        if k > 0:
            h_copy(k).wait_recv()
        for c in range(SLAB // 128):
            dots = dots + (sgr[slab(k), slab(c)].astype(jnp.float32)
                           * xs[k * T + c // 2, :, slab(c % 2)].astype(jnp.float32))
    rinv_own = rown[...]
    mean = jnp.sum(dots, axis=1, keepdims=True) * (1.0 / D) * rinv_own
    ab[...] = rinv_own
    bb[...] = rinv_own * rinv_own * mean

    @pl.when(p == 3)
    def _():
        pltpu.make_async_copy(cin, cin, lsem.at[5]).wait()

    def c_copy(n):
        part = slab(n, T)
        return rcopy(cout.at[part], cin.at[part], src_.at[n], rrc.at[n], ((p + 3) % 4, i))

    for n in range(CHUNKS):
        @pl.when(p < 3)
        def _():
            c_copy(n).wait_recv()

        a = wide(ab[...], ROWS)
        b = wide(bb[...], ROWS)
        for m in range(T):
            branch = (sgr[slab(n), slab(m, ROWS)].astype(jnp.float32) * a
                      - xs[n * T + m].astype(jnp.float32) * b)
            cout[n * T + m] = (cin[n * T + m].astype(jnp.float32) + branch).astype(jnp.bfloat16)

        @pl.when(p > 0)
        def _():
            c_copy(n).start()

        for m in range(T):
            pltpu.make_async_copy(
                cout.at[n * T + m], o_in.at[0, :, x_cols(n * T + m)], osem.at[1]).start()

    for k in range(1, T):
        ws_copy(k).wait_recv()
        gs_copy(k).wait_recv()

    gtotal = gs[0:1, :]
    total = wown[...]
    for k in range(1, T):
        total = total + wrecv[slab(k, ROWS), :].astype(jnp.float32)
        gtotal = gtotal + grecv[k * 8:k * 8 + 1, :]
    wown[...] = total
    o_gain[...] = gtotal
    out_k = pltpu.make_async_copy(wown.at[:, 0:KVW], o_kw.at[0], osem.at[2])
    out_v = pltpu.make_async_copy(wown.at[:, KVW:], o_vw.at[0], osem.at[3])
    out_k.start()
    out_v.start()

    for k in range(1, F):
        x_copy(k).wait_send()
        r_copy(k).wait_send()
        p_copy(k).wait_send()
        ga_copy(k).wait_send()
        h_copy(k).wait_send()
    for k in range(1, T):
        w_copy(k).wait_send()
        g_copy(k).wait_send()
        ws_copy(k).wait_send()
        gs_copy(k).wait_send()
    for copy in (hop1, hop2, even1, even2, back_a, back_b, back_c, back_d):
        copy.wait_send()

    @pl.when(p > 0)
    def _():
        for n in range(CHUNKS):
            c_copy(n).wait_send()

    pltpu.make_async_copy(cout, cout, osem.at[1]).wait()
    for copy in (out_q, out_k, out_v):
        copy.wait()


def on_device(layer_input, queries, out_grad, top_grad, norm_gain, key_weight, value_weight,
              weight_exponents, doc_lengths):
    factors = jnp.exp2(weight_exponents.astype(jnp.float32)).reshape(16)
    half = np.arange(128) % 64
    freq = np.power(np.float64(THETA), -(half * 2.0 / HEAD)).astype(np.float32)
    freq = jnp.asarray(np.broadcast_to(freq, (8, 128)))
    bf, f32 = jnp.bfloat16, jnp.float32
    vmem = functools.partial(pltpu.VMEM)
    dma = pltpu.SemaphoreType.DMA
    hbm = pl.BlockSpec(memory_space=pl.ANY)
    smem = pl.BlockSpec(memory_space=pltpu.SMEM)
    vm = pl.BlockSpec(memory_space=pltpu.VMEM)
    scratch = [
        vmem((F * T, TOK, ROWS), bf),
        vmem((F * T, TOK, ROWS), bf),
        vmem((ROWS, KVW), bf),
        vmem((ROWS, KVW), bf),
        vmem((SLAB, SLAB), bf),
        vmem((8 * T, ROWS), f32),
        vmem((64, 128), f32),
        vmem((TOK, 128), f32),
        vmem((QW, HEAD), bf),
        vmem((QW, HEAD), bf),
        vmem((F * T, TOK, ROWS), bf),
        vmem((F * T, TOK, ROWS), bf),
        vmem((TOK, 128), f32),
        vmem((TOK, 128), f32),
        vmem((WIN, 128), f32),
        vmem((SLAB, SLAB), bf),
        vmem((SLAB, SLAB), bf),
        vmem((SLAB, SLAB), bf),
        vmem((SLAB, SLAB), bf),
        vmem((WIN, SLAB), bf),
        vmem((WIN, SLAB), bf),
        vmem((WIN, SLAB), bf),
        vmem((WIN, SLAB), bf),
        vmem((4 * TOK, SLAB), bf),
        vmem((TOK, QW), bf),
        vmem((SLAB, SLAB), bf),
        vmem((SLAB, SLAB), bf),
        vmem((SLAB, SLAB), bf),
        vmem((TOK, 128), f32),
        vmem((TOK, 128), f32),
        vmem((SLAB, SLAB), bf),
        vmem((SLAB, SLAB), bf),
        vmem((ROWS, SLAB), f32),
        vmem((8 * T, ROWS), f32),
        vmem((8 * T, ROWS), f32),
        vmem((8, SLAB), f32),
        dma((6,)), dma((F,)), dma((F,)), dma((F,)), dma((F,)),
        dma((T,)), dma((T,)), dma((T,)), dma((T,)), dma((F,)), dma((F,)),
        dma((4,)), dma((4,)), dma((4,)), dma((4,)),
        dma((F,)), dma((F,)), dma((F,)), dma((F,)),
        dma((T,)), dma((T,)), dma((T,)), dma((T,)),
        dma((CHUNKS,)), dma((CHUNKS,)), dma((4,)),
    ]
    o_in, o_q, o_kw, o_vw, o_gain = pl.pallas_call(
        kernel,
        out_shape=(
            jax.ShapeDtypeStruct((1, TOK, D), bf),
            jax.ShapeDtypeStruct((1, TOK, QW), bf),
            jax.ShapeDtypeStruct((1, ROWS, KVW), f32),
            jax.ShapeDtypeStruct((1, ROWS, KVW), f32),
            jax.ShapeDtypeStruct((1, ROWS), f32),
        ),
        in_specs=[smem, smem, vm, hbm, hbm, hbm, hbm, vm, hbm, hbm],
        out_specs=(hbm, hbm, hbm, hbm, vm),
        scratch_shapes=scratch,
        compiler_params=pltpu.CompilerParams(
            collective_id=0, has_side_effects=True, vmem_limit_bytes=60 * 1024 * 1024),
    )(factors, doc_lengths, freq, layer_input, queries, out_grad, top_grad, norm_gain,
      key_weight, value_weight)
    return o_in, o_q, o_kw, o_vw, o_gain


def solution(mesh):
    in_specs = (
        P("pipe", "dp", None),
        P("pipe", "dp", None),
        P("pipe", "dp", None),
        P("dp", None),
        P("pipe", "dp"),
        P("pipe", "dp", None),
        P("pipe", "dp", None),
        P("pipe", None, "dp", None),
        P(),
    )
    out_specs = (
        P("pipe", "dp", None),
        P("pipe", "dp", None),
        P("pipe", "dp", None),
        P("pipe", "dp", None),
        P("pipe", "dp"),
    )
    return jax.shard_map(
        on_device, mesh=mesh, in_specs=in_specs, out_specs=out_specs, check_vma=False
    )
```

time: 971 us -> 215 us (0.22)
  waiting for transfers between devices: 555 us -> 0 us
  blocking collectives: 255 us -> 0 us
  Pallas kernels: 0 us -> 205 us
  matrix products: 56.6 us -> 0 us
  other arithmetic: 38.2 us -> 0.69 us
  starting transfers between devices: 22.3 us -> 0 us
  between operations: 15.9 us -> 0.66 us
  local copies, waits for them, and re-layouts: 21.4 us -> 8.19 us
    all_gather x2 -> x0, waiting for transfers between devices: 290 us -> none  [the longest x1 185 us: on_device(): lax.all_gather(key_local, 'dp', axis=0, tiled=True)]
    pallas_call x0 -> x1, Pallas kernels: none -> 205 us  [on_device(): pl.pallas_call(kernel, out_shape=(jax.ShapeDtypeStruct((1, TOK, D), bf),...]
    unnamed x1 -> x0, blocking collectives: 172 us -> none
    reduce_scatter x2 -> x0, waiting for transfers between devices: 168 us -> none  [the longest x1 168 us: on_device(): lax.psum_scatter(key_full_grad.astype(jnp.bfloat16), 'dp', scatter_dimens...]
    ppermute x11 -> x0, waiting for transfers between devices: 97.5 us -> none  [passed_along(): return lax.ppermute(block, axis, route)]
    all_gather x1 -> x0, blocking collectives: 82.9 us -> none  [on_device(): lax.all_gather(norm_gain[0], 'dp', axis=0, tiled=True)]
    dot_general x36 -> x0, matrix products: 56.6 us -> none  [the longest x1 6.42 us: on_device(): jnp.dot(hidden, key_full, preferred_element_type=jnp.float32)]
    ppermute x11 -> x0, starting transfers between devices: 22.1 us -> none  [passed_along(): return lax.ppermute(block, axis, route)]
  transfers between devices with their start and end apart: 15 -> 0, of which waited for: 9 -> 0; matrix products, arithmetic and copies ran while one was open for 7% -> 0% of each run, Pallas kernels for 0% -> 0%
where the time goes in v1:
time: 215 us
  Pallas kernels  205 us (95%)
  local copies, waits for them, and re-layouts  8.19 us (4%)
    pallas_call x1, Pallas kernels, on_device(): pl.pallas_call(kernel, out_shape=(jax.ShapeDtypeStruct((1, TOK, D), bf),...  205 us
    unnamed x13, local copies, waits for them, and re-layouts  6.35 us

profile of v1, /device:TPU:0, one launch (start us, length us, event | category | flops | bytes accessed | tf_op | source)
XLA Modules:
  0.0 214.7 jit_solution(16258161216876405967)
XLA Ops:
  0.6 0.7 multiply_exponential_fusion
  1.3 0.6 reshape.13.fac
  1.9 1.2 jit_solution_.3.freq
  3.2 205.1 %shard_map.137 = (bf16[1,128,8192]{2,1,0:T(8,128)(2,1)}, bf16[1,128,4096]{2,1,0:T(8,128)(2,1)}, f32[1,256,512]{2,1,0:T(8,128)}, f32[1,256,512]{2,1,0:T(8,128)}, f32[1,256]{1,0:T(1,128)}) custom-call(f32[16]{0:T(128)} %reshape.13.fac, s32[64]{0:T(128)} %docs.1, f32[8,128]{1,0:T(8,128)} %jit_solution_.3.freq, bf16[1,128,8192]{2,1,0:T(8,128)(2,1)} %x.1, ...), custom_call_target="tpu_custom_call" | custom-call | tf_op jit(solution)/shard_map/pallas_call | solution.py:542
  208.3 0.0 copy-start
  208.3 0.0 copy-start.2
  208.3 3.2 %copy.20 = bf16[1,128,8192]{2,1,0:T(8,128)(2,1)} copy(bf16[1,128,8192]{2,1,0:T(8,128)(2,1)} %get-tuple-element.10) | data formatting | bytes 4194304
  211.5 0.0 copy-done
  211.5 0.0 copy-start.1
  211.5 0.0 copy-start.3
  211.5 1.0 copy.21
  212.5 0.0 copy-done.2
  212.5 0.8 copy.22
  213.3 0.0 copy-done.1
  213.3 0.8 copy.23
  214.1 0.0 copy-done.3
  214.1 0.6 copy.24
Async XLA Ops:
  208.3 3.2 %copy-start = (bf16[1,128,4096]{2,1,0:T(8,128)(2,1)S(1)}, bf16[1,128,4096]{2,1,0:T(8,128)(2,1)}, u32[]{:S(2)}) copy-start(bf16[1,128,4096]{2,1,0:T(8,128)(2,1)} %get-tuple-element.11) | copy-start | bytes 3145732
  208.3 4.2 %copy-start.2 = (f32[1,256,512]{2,1,0:T(8,128)S(1)}, f32[1,256,512]{2,1,0:T(8,128)}, u32[]{:S(2)}) copy-start(f32[1,256,512]{2,1,0:T(8,128)} %get-tuple-element.12) | copy-start | bytes 1572868
  211.5 1.8 copy-start.1
  211.5 2.6 %copy-start.3 = (f32[1,256]{1,0:T(1,128)S(1)}, f32[1,256]{1,0:T(1,128)}, u32[]{:S(2)}) copy-start(f32[1,256]{1,0:T(1,128)} %get-tuple-element.14) | copy-start | bytes 3076

commit v2 on v1

--- a/solution.py
+++ b/solution.py
@@ -26,7 +26,6 @@
 T = 4
 SLAB = 1024
 WIN = (REACH + 1) * TOK
-CHUNKS = 8
 PAIR = 2
 
 MESH = pl.DeviceIdType.MESH
@@ -51,13 +50,13 @@
 
 
 def kernel(
-    fac, docs, freq, x, q, do, top, gain, kw, vw,
+    exps, docs, x, q, do, top, gain, kw, vw,
     o_in, o_q, o_kw, o_vw, o_gain,
     xs, xr, kwv, vwv, wr, gr, rr, rown, qs, dos, cin, cout, cosb, sinb, bias,
-    hbuf, ht, psend, precv, kwin, pt, dst, tb, ra, dq, gall, hgs, sgr, ab, bb,
+    hbuf, ht, proj, psend, precv, kwin, pt, dst, tb, ra, dq, gall, hgs, sgr, bb,
     ws, wrecv, wown, gs, grecv, gacc,
     lsem, sx, rx, sr, rrs, sw, rw, sg, rg, sp, rp, skv, rkv, sb, rb,
-    sga, rga, sh, rh, sws, rws, sgs, rgs, src_, rrc, osem,
+    sga, rga, sh, rh, sws, rws, sgs, rgs, src_, rrc, osem, lx,
 ):
     p = lax.axis_index("pipe")
     i = lax.axis_index("dp")
@@ -88,13 +87,86 @@
     def x_cols(n):
         return cols(((t + T - n % T) % T * F + (f + n // T) % F) * ROWS, ROWS)
 
-    def load_x(n, carry):
-        pltpu.make_async_copy(x.at[0, :, x_cols(n)], xs.at[n], lsem.at[0]).start()
-        return carry
-
-    lax.fori_loop(0, F * T, load_x, 0)
+    barrier = pltpu.get_barrier_semaphore()
+    peers = [f_up(k) for k in range(1, F)] + [t_up(k) for k in range(1, T)]
+    peers += [(p, (i + 2) % 32), (p, (i + 30) % 32)]
+    peers += [((p + 1) % 4, i), ((p + 3) % 4, i)]
+    for peer in peers:
+        pl.semaphore_signal(barrier, inc=1, device_id=peer, device_id_type=MESH)
+
+    def load_slab(k):
+        def load(n, carry):
+            pltpu.make_async_copy(
+                x.at[0, :, x_cols(k * T + n)], xs.at[k * T + n], lx.at[k]).start()
+            return carry
+
+        lax.fori_loop(0, T, load, 0)
+
+    order = list(range(1, F)) + [0]
+    load_slab(order[0])
     pltpu.make_async_copy(kw.at[0], kwv, lsem.at[1]).start()
     pltpu.make_async_copy(vw.at[0], vwv, lsem.at[2]).start()
+    for k in order[1:]:
+        load_slab(k)
+    pl.semaphore_wait(barrier, len(peers))
+
+    def x_copy(k):
+        return rcopy(xs.at[slab(k, T)], xr.at[slab(k, T)], sx.at[k], rx.at[k], f_up(k))
+
+    def wait_slab(k):
+        pltpu.make_async_copy(xs.at[slab(k, T)], xs.at[slab(k, T)], lx.at[k]).wait()
+
+    early = 3
+    for k in range(1, early):
+        wait_slab(k)
+        x_copy(k).start()
+
+    pltpu.make_async_copy(kw.at[0], kwv, lsem.at[1]).wait()
+    pltpu.make_async_copy(vw.at[0], vwv, lsem.at[2]).wait()
+    for rblock in range(2):
+        for cblock in range(4):
+            for which, wv in ((0, kwv), (1, vwv)):
+                block = wv[slab(rblock), slab(cblock)].astype(jnp.float32)
+                power = exps[which * 8 + rblock * 4 + cblock]
+                scaled = block * jnp.where(power > 0, 2.0, jnp.where(power < 0, 0.5, 1.0))
+                wr[slab(rblock), slab(which * 4 + cblock)] = scaled.astype(jnp.bfloat16)
+    gr[0:8, :] = jnp.broadcast_to(gain[...].astype(jnp.float32), (8, ROWS))
+
+    def w_copy(k):
+        return rcopy(wr.at[0:ROWS], wr.at[slab(k, ROWS)], sw.at[k], rw.at[k], t_up(k))
+
+    def g_copy(k):
+        return rcopy(gr.at[0:8], gr.at[slab(k, 8)], sg.at[k], rg.at[k], t_up(k))
+
+    for k in range(1, T):
+        g_copy(k).start()
+        w_copy(k).start()
+
+    for k in range(early, F):
+        wait_slab(k)
+    wait_slab(0)
+
+    def add_squares(n, acc):
+        part = xs[n].astype(jnp.float32)
+        part = part * part
+        for c in range(ROWS // 128):
+            acc = acc + part[:, slab(c)]
+        return acc
+
+    squares = lax.fori_loop(0, F * T, add_squares, jnp.zeros((TOK, 128), jnp.float32))
+    mean_sq = jnp.sum(squares, axis=1, keepdims=True) * (1.0 / D)
+    rinv = jnp.broadcast_to(1.0 / jnp.sqrt(mean_sq + EPS), (TOK, 128))
+    rown[...] = rinv
+    rr[0:8, :] = rinv.T[0:8, :]
+
+    def r_copy(k):
+        return rcopy(rr.at[0:8], rr.at[slab(k, 8)], sr.at[k], rrs.at[k], f_up(k))
+
+    for k in range(1, F):
+        r_copy(k).start()
+    for k in range(early, F):
+        x_copy(k).start()
+    xr[0:T] = xs[0:T]
 
     def load_q(n, carry):
         pltpu.make_async_copy(
@@ -113,62 +185,6 @@
 
         lax.fori_loop(0, F * T, load_top, 0)
 
-    barrier = pltpu.get_barrier_semaphore()
-    peers = [f_up(k) for k in range(1, F)] + [t_up(k) for k in range(1, T)]
-    peers += [(p, (i + 2) % 32), (p, (i + 30) % 32)]
-    peers += [((p + 1) % 4, i), ((p + 3) % 4, i)]
-    for peer in peers:
-        pl.semaphore_signal(barrier, inc=1, device_id=peer, device_id_type=MESH)
-    pl.semaphore_wait(barrier, len(peers))
-
-    pltpu.make_async_copy(xs, xs, lsem.at[0]).wait()
-
-    def x_copy(k):
-        return rcopy(xs.at[slab(k, T)], xr.at[slab(k, T)], sx.at[k], rx.at[k], f_up(k))
-
-    for k in range(1, F):
-        x_copy(k).start()
-    xr[0:T] = xs[0:T]
-
-    pltpu.make_async_copy(kw.at[0], kwv, lsem.at[1]).wait()
-    pltpu.make_async_copy(vw.at[0], vwv, lsem.at[2]).wait()
-    for rblock in range(2):
-        for cblock in range(4):
-            for which, wv in ((0, kwv), (1, vwv)):
-                block = wv[slab(rblock), slab(cblock)].astype(jnp.float32)
-                scaled = block * fac[which * 8 + rblock * 4 + cblock]
-                wr[slab(rblock), slab(which * 4 + cblock)] = scaled.astype(jnp.bfloat16)
-    gr[0:8, :] = jnp.broadcast_to(gain[...].astype(jnp.float32), (8, ROWS))
-
-    def w_copy(k):
-        return rcopy(wr.at[0:ROWS], wr.at[slab(k, ROWS)], sw.at[k], rw.at[k], t_up(k))
-
-    def g_copy(k):
-        return rcopy(gr.at[0:8], gr.at[slab(k, 8)], sg.at[k], rg.at[k], t_up(k))
-
-    for k in range(1, T):
-        w_copy(k).start()
-        g_copy(k).start()
-
-    def add_squares(n, acc):
-        part = xs[n].astype(jnp.float32)
-        part = part * part
-        for c in range(ROWS // 128):
-            acc = acc + part[:, slab(c)]
-        return acc
-
-    squares = lax.fori_loop(0, F * T, add_squares, jnp.zeros((TOK, 128), jnp.float32))
-    mean_sq = jnp.sum(squares, axis=1, keepdims=True) * (1.0 / D)
-    rinv = jnp.broadcast_to(1.0 / jnp.sqrt(mean_sq + EPS), (TOK, 128))
-    rown[...] = rinv
-    rr[0:8, :] = rinv.T[0:8, :]
-
-    def r_copy(k):
-        return rcopy(rr.at[0:8], rr.at[slab(k, 8)], sr.at[k], rrs.at[k], f_up(k))
-
-    for k in range(1, F):
-        r_copy(k).start()
-
     tok_col = i * TOK + lax.broadcasted_iota(jnp.int32, (TOK, 128), 0)
     tok_row = i * TOK + lax.broadcasted_iota(jnp.int32, (8, 128), 1)
 
@@ -181,8 +197,12 @@
     _, scol, srow = lax.fori_loop(
         0, 64, scan_docs,
         (jnp.int32(0), jnp.zeros((TOK, 128), jnp.int32), jnp.zeros((8, 128), jnp.int32)))
-    angle = (tok_col - scol).astype(jnp.float32) * freq[0:1, :]
     lane = lax.broadcasted_iota(jnp.int32, (TOK, 128), 1)
+    freq = jnp.ones((TOK, 128), jnp.float32)
+    for bit in range(6):
+        power = float(np.float64(THETA) ** (-(2.0 * 2 ** bit / HEAD)))
+        freq = jnp.where((lane & (1 << bit)) != 0, freq * power, freq)
+    angle = (tok_col - scol).astype(jnp.float32) * freq
     sine = jnp.sin(angle)
     cosb[...] = jnp.cos(angle)
     sinb[...] = jnp.where(lane < 64, -sine, sine)
@@ -233,7 +253,10 @@
         for k in range(1, F):
             total = total + precv[slab(k), slab(c)].astype(jnp.float32)
         if c < 4:
+            proj[:, slab(c)] = total
             total = rope(total, 1.0)
+        else:
+            proj[:, slab(c)] = total
         kwin[REACH * TOK:, slab(c)] = total.astype(jnp.bfloat16)
 
     partner = (p, i + 1 - 2 * xl)
@@ -352,18 +375,25 @@
     out_q = pltpu.make_async_copy(dq, o_q.at[0], osem.at[0])
     out_q.start()
     back_d.wait_recv()
+    dots = jnp.zeros((TOK, 128), jnp.float32)
     for c in range(8):
         total = (tb[slab(REACH), slab(c)].astype(jnp.float32)
                  + ra[slab(3), slab(c)].astype(jnp.float32))
         if c < 4:
             total = rope(total, -1.0)
-        gall[0:TOK, slab(c)] = total.astype(jnp.bfloat16)
+        total = total.astype(jnp.bfloat16)
+        gall[0:TOK, slab(c)] = total
+        dots = dots + total.astype(jnp.float32) * proj[:, slab(c)]
 
     def ga_copy(k):
         return rcopy(gall.at[0:TOK], gall.at[slab(k)], sga.at[k], rga.at[k], f_up(k))
 
     for k in range(1, F):
         ga_copy(k).start()
+
+    rinv_own = rown[...]
+    mean = jnp.sum(dots, axis=1, keepdims=True) * (1.0 / D)
+    bb[...] = rinv_own * rinv_own * mean
 
     gacc[...] = jnp.zeros_like(gacc)
 
@@ -397,23 +427,13 @@
         return rcopy(ws.at[slab(k, ROWS)], wrecv.at[slab(k, ROWS)], sws.at[k], rws.at[k],
                      t_down(k))
 
-    for k in range(1, T):
-        ws[slab(k, ROWS), :] = dot(ht[slab(k, ROWS), :], gall[...]).astype(jnp.bfloat16)
-        ws_copy(k).start()
-        gs_copy(k).start()
-    wown[...] = dot(ht[0:ROWS, :], gall[...])
-
-    dots = jnp.zeros((TOK, 128), jnp.float32)
-    for k in range(F):
-        if k > 0:
-            h_copy(k).wait_recv()
-        for c in range(SLAB // 128):
-            dots = dots + (sgr[slab(k), slab(c)].astype(jnp.float32)
-                           * xs[k * T + c // 2, :, slab(c % 2)].astype(jnp.float32))
-    rinv_own = rown[...]
-    mean = jnp.sum(dots, axis=1, keepdims=True) * (1.0 / D) * rinv_own
-    ab[...] = rinv_own
-    bb[...] = rinv_own * rinv_own * mean
+    def weight_term(k):
+        if k == 0:
+            wown[...] = dot(ht[0:ROWS, :], gall[...])
+        else:
+            ws[slab(k, ROWS), :] = dot(ht[slab(k, ROWS), :], gall[...]).astype(jnp.bfloat16)
+            ws_copy(k).start()
+            gs_copy(k).start()
 
     @pl.when(p == 3)
     def _():
@@ -423,12 +443,15 @@
         part = slab(n, T)
         return rcopy(cout.at[part], cin.at[part], src_.at[n], rrc.at[n], ((p + 3) % 4, i))
 
-    for n in range(CHUNKS):
+    for n in range(F):
+        if n > 0:
+            h_copy(n).wait_recv()
+
         @pl.when(p < 3)
         def _():
             c_copy(n).wait_recv()
 
-        a = wide(ab[...], ROWS)
+        a = wide(rown[...], ROWS)
         b = wide(bb[...], ROWS)
         for m in range(T):
             branch = (sgr[slab(n), slab(m, ROWS)].astype(jnp.float32) * a
@@ -442,6 +465,8 @@
         for m in range(T):
             pltpu.make_async_copy(
                 cout.at[n * T + m], o_in.at[0, :, x_cols(n * T + m)], osem.at[1]).start()
+        if n < T:
+            weight_term((n + 1) % T)
 
     for k in range(1, T):
         ws_copy(k).wait_recv()
@@ -475,7 +500,7 @@
 
     @pl.when(p > 0)
     def _():
-        for n in range(CHUNKS):
+        for n in range(F):
             c_copy(n).wait_send()
 
     pltpu.make_async_copy(cout, cout, osem.at[1]).wait()
@@ -485,10 +510,6 @@
 
 def on_device(layer_input, queries, out_grad, top_grad, norm_gain, key_weight, value_weight,
               weight_exponents, doc_lengths):
-    factors = jnp.exp2(weight_exponents.astype(jnp.float32)).reshape(16)
-    half = np.arange(128) % 64
-    freq = np.power(np.float64(THETA), -(half * 2.0 / HEAD)).astype(np.float32)
-    freq = jnp.asarray(np.broadcast_to(freq, (8, 128)))
     bf, f32 = jnp.bfloat16, jnp.float32
     vmem = functools.partial(pltpu.VMEM)
     dma = pltpu.SemaphoreType.DMA
@@ -513,6 +534,7 @@
         vmem((WIN, 128), f32),
         vmem((SLAB, SLAB), bf),
         vmem((SLAB, SLAB), bf),
+        vmem((TOK, SLAB), f32),
         vmem((SLAB, SLAB), bf),
         vmem((SLAB, SLAB), bf),
         vmem((WIN, SLAB), bf),
@@ -524,7 +546,6 @@
         vmem((SLAB, SLAB), bf),
         vmem((SLAB, SLAB), bf),
         vmem((SLAB, SLAB), bf),
-        vmem((TOK, 128), f32),
         vmem((TOK, 128), f32),
         vmem((SLAB, SLAB), bf),
         vmem((SLAB, SLAB), bf),
@@ -537,7 +558,7 @@
         dma((4,)), dma((4,)), dma((4,)), dma((4,)),
         dma((F,)), dma((F,)), dma((F,)), dma((F,)),
         dma((T,)), dma((T,)), dma((T,)), dma((T,)),
-        dma((CHUNKS,)), dma((CHUNKS,)), dma((4,)),
+        dma((F,)), dma((F,)), dma((4,)), dma((F,)),
     ]
     o_in, o_q, o_kw, o_vw, o_gain = pl.pallas_call(
         kernel,
@@ -548,12 +569,12 @@
             jax.ShapeDtypeStruct((1, ROWS, KVW), f32),
             jax.ShapeDtypeStruct((1, ROWS), f32),
         ),
-        in_specs=[smem, smem, vm, hbm, hbm, hbm, hbm, vm, hbm, hbm],
+        in_specs=[smem, smem, hbm, hbm, hbm, hbm, vm, hbm, hbm],
         out_specs=(hbm, hbm, hbm, hbm, vm),
         scratch_shapes=scratch,
         compiler_params=pltpu.CompilerParams(
             collective_id=0, has_side_effects=True, vmem_limit_bytes=60 * 1024 * 1024),
-    )(factors, doc_lengths, freq, layer_input, queries, out_grad, top_grad, norm_gain,
+    )(weight_exponents.reshape(16), doc_lengths, layer_input, queries, out_grad, top_grad, norm_gain,
       key_weight, value_weight)
     return o_in, o_q, o_kw, o_vw, o_gain
 

time: 215 us -> 217 us (level)
  the two profiles are of different devices: /device:TPU:0 before, /device:TPU:3 now
where the time goes in v2:
time: 217 us
  Pallas kernels  208 us (96%)
  local copies, waits for them, and re-layouts  7.62 us (4%)
    pallas_call x1, Pallas kernels, on_device(): pl.pallas_call(kernel, out_shape=(jax.ShapeDtypeStruct((1, TOK, D), bf),...  208 us
    unnamed x13, local copies, waits for them, and re-layouts  6.35 us

profile of v2, /device:TPU:3, one launch (start us, length us, event | category | flops | bytes accessed | tf_op | source)
XLA Modules:
  0.0 216.7 jit_solution(6816597835947112646)
XLA Ops:
  0.6 1.3 reshape.13.exps
  1.9 208.5 %shard_map.128 = (bf16[1,128,8192]{2,1,0:T(8,128)(2,1)}, bf16[1,128,4096]{2,1,0:T(8,128)(2,1)}, f32[1,256,512]{2,1,0:T(8,128)}, f32[1,256,512]{2,1,0:T(8,128)}, f32[1,256]{1,0:T(1,128)}) custom-call(s32[16]{0:T(128)} %reshape.13.exps, s32[64]{0:T(128)} %docs.1, bf16[1,128,8192]{2,1,0:T(8,128)(2,1)} %x.1, bf16[1,128,4096]{2,1,0:T(8,128)(2,1)} %q.1, ...), custom_call_target="tpu_custom_call" | custom-call | tf_op jit(solution)/shard_map/pallas_call | solution.py:563
  210.4 0.0 copy-start
  210.4 0.0 copy-start.2
  210.4 3.2 %copy.19 = bf16[1,128,8192]{2,1,0:T(8,128)(2,1)} copy(bf16[1,128,8192]{2,1,0:T(8,128)(2,1)} %get-tuple-element.10) | data formatting | bytes 4194304
  213.6 0.0 copy-done
  213.6 0.0 copy-start.1
  213.6 0.0 copy-start.3
  213.6 1.0 copy.20
  214.6 0.0 copy-done.2
  214.6 0.8 copy.21
  215.4 0.0 copy-done.1
  215.4 0.8 copy.22
  216.2 0.0 copy-done.3
  216.2 0.6 copy.23
Async XLA Ops:
  210.4 3.2 %copy-start = (bf16[1,128,4096]{2,1,0:T(8,128)(2,1)S(1)}, bf16[1,128,4096]{2,1,0:T(8,128)(2,1)}, u32[]{:S(2)}) copy-start(bf16[1,128,4096]{2,1,0:T(8,128)(2,1)} %get-tuple-element.11) | copy-start | bytes 3145732
  210.4 4.2 %copy-start.2 = (f32[1,256,512]{2,1,0:T(8,128)S(1)}, f32[1,256,512]{2,1,0:T(8,128)}, u32[]{:S(2)}) copy-start(f32[1,256,512]{2,1,0:T(8,128)} %get-tuple-element.12) | copy-start | bytes 1572868
  213.6 1.8 copy-start.1
  213.6 2.6 %copy-start.3 = (f32[1,256]{1,0:T(1,128)S(1)}, f32[1,256]{1,0:T(1,128)}, u32[]{:S(2)}) copy-start(f32[1,256]{1,0:T(1,128)} %get-tuple-element.14) | copy-start | bytes 3076

commit v3 on v2

--- a/solution.py
+++ b/solution.py
@@ -127,9 +127,10 @@
         for cblock in range(4):
             for which, wv in ((0, kwv), (1, vwv)):
                 block = wv[slab(rblock), slab(cblock)].astype(jnp.float32)
-                power = exps[which * 8 + rblock * 4 + cblock]
+                power = exps[0, which, rblock, cblock]
+                place = cblock // 2 * 4 + which * 2 + cblock % 2
                 scaled = block * jnp.where(power > 0, 2.0, jnp.where(power < 0, 0.5, 1.0))
-                wr[slab(rblock), slab(which * 4 + cblock)] = scaled.astype(jnp.bfloat16)
+                wr[slab(rblock), slab(place)] = scaled.astype(jnp.bfloat16)
     gr[0:8, :] = jnp.broadcast_to(gain[...].astype(jnp.float32), (8, ROWS))
 
     def w_copy(k):
@@ -223,8 +224,12 @@
 
     gain_row = jnp.concatenate([gr[n * 8:n * 8 + 1, :] for n in range(T)], axis=1)
 
-    def p_copy(k):
-        return rcopy(psend.at[slab(k)], precv.at[slab(k)], sp.at[k], rp.at[k], f_down(k))
+    def half_slab(u, k):
+        return slab(u * F + k)
+
+    def p_copy(u, k):
+        return rcopy(psend.at[half_slab(u, k)], precv.at[half_slab(u, k)],
+                     sp.at[u * F + k], rp.at[u * F + k], f_down(k))
 
     for k in range(F):
         if k > 0:
@@ -233,83 +238,97 @@
         hidden = (slab_x(k) * wide(inv_rms(k), SLAB) * gain_row).astype(jnp.bfloat16)
         hbuf[slab(k), :] = hidden
         part = dot(hidden, wr[...]).astype(jnp.bfloat16)
+        for u in range(2):
+            target = psend if k > 0 else precv
+            target[half_slab(u, k), :] = part[:, slab(u, KVW)]
         if k > 0:
-            psend[slab(k), :] = part
-            p_copy(k).start()
-        else:
-            precv[slab(k), :] = part
+            p_copy(0, k).start()
+    for k in range(1, F):
+        p_copy(1, k).start()
 
     for k in range(F):
         ht[:, slab(k)] = hbuf[slab(k), :].T
 
-    for k in range(1, F):
-        p_copy(k).wait_recv()
-
     def rope(block, sign):
         return block * cosb[...] + pltpu.roll(block, 64, 1) * (sinb[...] * sign)
-
-    for c in range(8):
-        total = precv[0:TOK, slab(c)].astype(jnp.float32)
-        for k in range(1, F):
-            total = total + precv[slab(k), slab(c)].astype(jnp.float32)
-        if c < 4:
-            proj[:, slab(c)] = total
-            total = rope(total, 1.0)
-        else:
-            proj[:, slab(c)] = total
-        kwin[REACH * TOK:, slab(c)] = total.astype(jnp.bfloat16)
 
     partner = (p, i + 1 - 2 * xl)
     ahead = (p, (i + 2) % 32)
     back = (p, (i + 30) % 32)
 
-    def kv_copy(src, dst_slot, n, dev):
-        return rcopy(kwin.at[slab(src)], kwin.at[slab(dst_slot)], skv.at[n], rkv.at[n], dev)
-
-    hop1 = kv_copy(4, 2, 0, ahead)
-    hop2 = kv_copy(2, 0, 1, ahead)
-    even1 = kv_copy(4, 3, 2, partner)
-    even2 = kv_copy(2, 1, 3, partner)
-    odd1 = kv_copy(2, 3, 2, partner)
-    odd2 = kv_copy(0, 1, 3, partner)
-    hop1.start()
-
-    @pl.when(xl == 0)
-    def _():
-        even1.start()
-
-    hop1.wait_recv()
-    hop2.start()
-
-    @pl.when(xl == 0)
-    def _():
-        even2.start()
-
-    @pl.when(xl == 1)
-    def _():
-        odd1.start()
-
-    hop2.wait_recv()
-
-    @pl.when(xl == 1)
-    def _():
-        odd2.start()
-
-    pltpu.make_async_copy(qs, qs, lsem.at[3]).wait()
-    pltpu.make_async_copy(dos, dos, lsem.at[4]).wait()
-    even1.wait_recv()
-    even2.wait_recv()
+    def slot(u, s):
+        return slab(u * (REACH + 1) + s)
+
+    def own_block(u):
+        for k in range(1, F):
+            p_copy(u, k).wait_recv()
+        for c in range(4):
+            total = precv[half_slab(u, 0), slab(c)].astype(jnp.float32)
+            for k in range(1, F):
+                total = total + precv[half_slab(u, k), slab(c)].astype(jnp.float32)
+            proj[:, slab(u * 4 + c)] = total
+            if c < 2:
+                total = rope(total, 1.0)
+            kwin[slot(u, REACH), slab(c)] = total.astype(jnp.bfloat16)
+
+    class Window:
+        def __init__(self, u):
+            def copy(src, dst_slot, n, dev):
+                return rcopy(kwin.at[slot(u, src)], kwin.at[slot(u, dst_slot)],
+                             skv.at[u * 4 + n], rkv.at[u * 4 + n], dev)
+
+            self.hop1 = copy(4, 2, 0, ahead)
+            self.hop2 = copy(2, 0, 1, ahead)
+            self.even1 = copy(4, 3, 2, partner)
+            self.even2 = copy(2, 1, 3, partner)
+            self.odd1 = copy(2, 3, 2, partner)
+            self.odd2 = copy(0, 1, 3, partner)
+
+        def first(self):
+            self.hop1.start()
+
+            @pl.when(xl == 0)
+            def _():
+                self.even1.start()
+
+        def second(self):
+            self.hop1.wait_recv()
+            self.hop2.start()
+
+            @pl.when(xl == 0)
+            def _():
+                self.even2.start()
+
+            @pl.when(xl == 1)
+            def _():
+                self.odd1.start()
+
+        def third(self):
+            self.hop2.wait_recv()
+
+            @pl.when(xl == 1)
+            def _():
+                self.odd2.start()
+
+        def last(self):
+            self.even1.wait_recv()
+            self.even2.wait_recv()
+
+        def sent(self):
+            for copy in (self.hop1, self.hop2, self.even1, self.even2):
+                copy.wait_send()
 
     inv_root = 1.0 / math.sqrt(HEAD)
-
-    def one_kv_head(h, carry):
-        kcol = cols(h * HEAD, HEAD)
-        vcol = cols(KVW + h * HEAD, HEAD)
-        keys = kwin[:, kcol]
-        vals = kwin[:, vcol]
+    steps = Q_PER_KV // PAIR
+
+    def attend(h, first, last):
+        u, c = h // 2, h % 2
+        window = slice(u * WIN, (u + 1) * WIN)
+        keys = kwin[window, slab(c)]
+        vals = kwin[window, slab(2 + c)]
         keys_t = keys.T
 
-        def heads(g, carry2):
+        def heads(g, carry):
             width = PAIR * TOK
             qrow = rows((h * Q_PER_KV + g * PAIR) * TOK, width)
             scores = dot(keys, qs[qrow, :], NT) * inv_root + wide(bias[...], width)
@@ -327,70 +346,120 @@
             for n in range(PAIR):
                 head = (h * Q_PER_KV + g * PAIR + n) * HEAD
                 dq[:, cols(head, HEAD)] = dqt[:, slab(n)].T.astype(jnp.bfloat16)
-            return carry2
-
-        lax.fori_loop(0, Q_PER_KV // PAIR, heads, 0)
-        hrow = rows(h * Q_PER_KV * TOK, Q_PER_KV * TOK)
-        tb[:, vcol] = dot(pt[...], dos[hrow, :]).astype(jnp.bfloat16)
-        tb[:, kcol] = (dot(dst[...], qs[hrow, :]) * inv_root).astype(jnp.bfloat16)
-        return carry
-
-    lax.fori_loop(0, KV_HEADS, one_kv_head, 0)
-
-    def t_copy(src, n, dev):
-        return rcopy(tb.at[slab(src)], ra.at[slab(n)], sb.at[n], rb.at[n], dev)
-
-    back_a = t_copy(3, 0, partner)
-    back_b = t_copy(1, 1, partner)
-    back_c = t_copy(0, 2, back)
-    back_d = t_copy(2, 3, back)
-    back_b.start()
-    back_a.start()
-
-    def fold(s, n):
-        tb[slab(s), :] = (tb[slab(s), :].astype(jnp.float32)
-                          + ra[slab(n), :].astype(jnp.float32)).astype(jnp.bfloat16)
-
-    back_b.wait_recv()
-
-    @pl.when(xl == 1)
-    def _():
-        fold(0, 1)
-
-    back_c.start()
-    back_a.wait_recv()
-
-    @pl.when(xl == 1)
-    def _():
-        fold(2, 0)
-
-    @pl.when(xl == 0)
-    def _():
-        fold(2, 1)
-        fold(4, 0)
-
-    back_c.wait_recv()
-    fold(2, 2)
-    back_d.start()
+            return carry
+
+        lax.fori_loop(first, last, heads, 0)
+        if last == steps:
+            hrow = slab(h, Q_PER_KV * TOK)
+            tb[window, slab(2 + c)] = dot(pt[...], dos[hrow, :]).astype(jnp.bfloat16)
+            tb[window, slab(c)] = (dot(dst[...], qs[hrow, :]) * inv_root).astype(jnp.bfloat16)
+
+    class Terms:
+        def __init__(self, u):
+            def copy(src, n, dev):
+                return rcopy(tb.at[slot(u, src)], ra.at[slab(u * 4 + n)],
+                             sb.at[u * 4 + n], rb.at[u * 4 + n], dev)
+
+            self.u = u
+            self.a = copy(3, 0, partner)
+            self.b = copy(1, 1, partner)
+            self.c = copy(0, 2, back)
+            self.d = copy(2, 3, back)
+
+        def fold(self, s, n):
+            at = slot(self.u, s)
+            tb[at, :] = (tb[at, :].astype(jnp.float32)
+                         + ra[slab(self.u * 4 + n), :].astype(jnp.float32)).astype(jnp.bfloat16)
+
+        def first(self):
+            @pl.when(xl == 0)
+            def _():
+                self.c.start()
+
+            self.b.start()
+            self.a.start()
+
+        def second(self):
+            self.b.wait_recv()
+
+            @pl.when(xl == 1)
+            def _():
+                self.fold(0, 1)
+                self.c.start()
+
+            self.a.wait_recv()
+
+            @pl.when(xl == 1)
+            def _():
+                self.fold(2, 0)
+
+            @pl.when(xl == 0)
+            def _():
+                self.fold(2, 1)
+                self.fold(4, 0)
+
+        def third(self):
+            self.c.wait_recv()
+            self.fold(2, 2)
+            self.d.start()
+
+        def last(self):
+            u = self.u
+            self.d.wait_recv()
+            for c in range(4):
+                total = (tb[slot(u, REACH), slab(c)].astype(jnp.float32)
+                         + ra[slab(u * 4 + 3), slab(c)].astype(jnp.float32))
+                if c < 2:
+                    total = rope(total, -1.0)
+                gall[half_slab(u, 0), slab(c)] = total.astype(jnp.bfloat16)
+            for k in range(1, F):
+                ga_copy(u, k).start()
+
+        def sent(self):
+            for copy in (self.a, self.b, self.c, self.d):
+                copy.wait_send()
+
+    def ga_copy(u, k):
+        return rcopy(gall.at[half_slab(u, 0)], gall.at[half_slab(u, k)],
+                     sga.at[u * F + k], rga.at[u * F + k], f_up(k))
+
+    windows = [Window(0), Window(1)]
+    terms = [Terms(0), Terms(1)]
+    own_block(0)
+    windows[0].first()
+    pltpu.make_async_copy(qs, qs, lsem.at[3]).wait()
+    pltpu.make_async_copy(dos, dos, lsem.at[4]).wait()
+    windows[0].second()
+    windows[0].third()
+    own_block(1)
+    windows[1].first()
+    windows[0].last()
+    attend(0, 0, steps // 2)
+    windows[1].second()
+    attend(0, steps // 2, steps)
+    attend(1, 0, steps // 2)
+    windows[1].third()
+    attend(1, steps // 2, steps)
+    terms[0].first()
+    windows[1].last()
+    attend(2, 0, steps)
+    terms[0].second()
+    attend(3, 0, steps // 2)
+    terms[0].third()
+    attend(3, steps // 2, steps)
+    terms[1].first()
     out_q = pltpu.make_async_copy(dq, o_q.at[0], osem.at[0])
     out_q.start()
-    back_d.wait_recv()
+    terms[0].last()
+    terms[1].second()
+    terms[1].third()
+    terms[1].last()
+
     dots = jnp.zeros((TOK, 128), jnp.float32)
-    for c in range(8):
-        total = (tb[slab(REACH), slab(c)].astype(jnp.float32)
-                 + ra[slab(3), slab(c)].astype(jnp.float32))
-        if c < 4:
-            total = rope(total, -1.0)
-        total = total.astype(jnp.bfloat16)
-        gall[0:TOK, slab(c)] = total
-        dots = dots + total.astype(jnp.float32) * proj[:, slab(c)]
-
-    def ga_copy(k):
-        return rcopy(gall.at[0:TOK], gall.at[slab(k)], sga.at[k], rga.at[k], f_up(k))
-
-    for k in range(1, F):
-        ga_copy(k).start()
-
+    for u in range(2):
+        for c in range(4):
+            dots = dots + (gall[half_slab(u, 0), slab(c)].astype(jnp.float32)
+                           * proj[:, slab(u * 4 + c)])
     rinv_own = rown[...]
     mean = jnp.sum(dots, axis=1, keepdims=True) * (1.0 / D)
     bb[...] = rinv_own * rinv_own * mean
@@ -402,8 +471,10 @@
 
     for k in range(F):
         if k > 0:
-            ga_copy(k).wait_recv()
-        hg = dot(gall[slab(k), :], wr[...], NT)
+            ga_copy(0, k).wait_recv()
+            ga_copy(1, k).wait_recv()
+        hg = (dot(gall[half_slab(0, k), :], wr[:, 0:KVW], NT)
+              + dot(gall[half_slab(1, k), :], wr[:, KVW:], NT))
         scaled = (hg * gain_row).astype(jnp.bfloat16)
         if k > 0:
             hgs[slab(k), :] = scaled
@@ -428,10 +499,13 @@
                      t_down(k))
 
     def weight_term(k):
-        if k == 0:
-            wown[...] = dot(ht[0:ROWS, :], gall[...])
-        else:
-            ws[slab(k, ROWS), :] = dot(ht[slab(k, ROWS), :], gall[...]).astype(jnp.bfloat16)
+        for u in range(2):
+            term = dot(ht[slab(k, ROWS), :], gall[slab(u, SLAB), :])
+            if k == 0:
+                wown[:, slab(u, KVW)] = term
+            else:
+                ws[slab(k, ROWS), slab(u, KVW)] = term.astype(jnp.bfloat16)
+        if k > 0:
             ws_copy(k).start()
             gs_copy(k).start()
 
@@ -479,24 +553,28 @@
         gtotal = gtotal + grecv[k * 8:k * 8 + 1, :]
     wown[...] = total
     o_gain[...] = gtotal
-    out_k = pltpu.make_async_copy(wown.at[:, 0:KVW], o_kw.at[0], osem.at[2])
-    out_v = pltpu.make_async_copy(wown.at[:, KVW:], o_vw.at[0], osem.at[3])
-    out_k.start()
-    out_v.start()
+    outs = []
+    for u in range(2):
+        for which, out in ((0, o_kw), (1, o_vw)):
+            outs.append(pltpu.make_async_copy(
+                wown.at[:, slab(u * 2 + which, 256)], out.at[0, :, slab(u, 256)],
+                osem.at[2 + u * 2 + which]))
+            outs[-1].start()
 
     for k in range(1, F):
         x_copy(k).wait_send()
         r_copy(k).wait_send()
-        p_copy(k).wait_send()
-        ga_copy(k).wait_send()
+        for u in range(2):
+            p_copy(u, k).wait_send()
+            ga_copy(u, k).wait_send()
         h_copy(k).wait_send()
     for k in range(1, T):
         w_copy(k).wait_send()
         g_copy(k).wait_send()
         ws_copy(k).wait_send()
         gs_copy(k).wait_send()
-    for copy in (hop1, hop2, even1, even2, back_a, back_b, back_c, back_d):
-        copy.wait_send()
+    for member in windows + terms:
+        member.sent()
 
     @pl.when(p > 0)
     def _():
@@ -504,7 +582,7 @@
             c_copy(n).wait_send()
 
     pltpu.make_async_copy(cout, cout, osem.at[1]).wait()
-    for copy in (out_q, out_k, out_v):
+    for copy in [out_q] + outs:
         copy.wait()
 
 
@@ -535,15 +613,15 @@
         vmem((SLAB, SLAB), bf),
         vmem((SLAB, SLAB), bf),
         vmem((TOK, SLAB), f32),
-        vmem((SLAB, SLAB), bf),
-        vmem((SLAB, SLAB), bf),
+        vmem((2 * SLAB, KVW), bf),
+        vmem((2 * SLAB, KVW), bf),
+        vmem((2 * WIN, KVW), bf),
         vmem((WIN, SLAB), bf),
         vmem((WIN, SLAB), bf),
-        vmem((WIN, SLAB), bf),
-        vmem((WIN, SLAB), bf),
-        vmem((4 * TOK, SLAB), bf),
+        vmem((2 * WIN, KVW), bf),
+        vmem((8 * TOK, KVW), bf),
         vmem((TOK, QW), bf),
-        vmem((SLAB, SLAB), bf),
+        vmem((2 * SLAB, KVW), bf),
         vmem((SLAB, SLAB), bf),
         vmem((SLAB, SLAB), bf),
         vmem((TOK, 128), f32),
@@ -554,11 +632,11 @@
         vmem((8 * T, ROWS), f32),
         vmem((8, SLAB), f32),
         dma((6,)), dma((F,)), dma((F,)), dma((F,)), dma((F,)),
-        dma((T,)), dma((T,)), dma((T,)), dma((T,)), dma((F,)), dma((F,)),
-        dma((4,)), dma((4,)), dma((4,)), dma((4,)),
-        dma((F,)), dma((F,)), dma((F,)), dma((F,)),
+        dma((T,)), dma((T,)), dma((T,)), dma((T,)), dma((2 * F,)), dma((2 * F,)),
+        dma((8,)), dma((8,)), dma((8,)), dma((8,)),
+        dma((2 * F,)), dma((2 * F,)), dma((F,)), dma((F,)),
         dma((T,)), dma((T,)), dma((T,)), dma((T,)),
-        dma((F,)), dma((F,)), dma((4,)), dma((F,)),
+        dma((F,)), dma((F,)), dma((6,)), dma((F,)),
     ]
     o_in, o_q, o_kw, o_vw, o_gain = pl.pallas_call(
         kernel,
@@ -574,7 +652,7 @@
         scratch_shapes=scratch,
         compiler_params=pltpu.CompilerParams(
             collective_id=0, has_side_effects=True, vmem_limit_bytes=60 * 1024 * 1024),
-    )(weight_exponents.reshape(16), doc_lengths, layer_input, queries, out_grad, top_grad, norm_gain,
+    )(weight_exponents, doc_lengths, layer_input, queries, out_grad, top_grad, norm_gain,
       key_weight, value_weight)
     return o_in, o_q, o_kw, o_vw, o_gain
 

time: 217 us -> 193 us (0.89)
  the two profiles are of different devices: /device:TPU:3 before, /device:TPU:0 now
where the time goes in v3:
time: 193 us
  Pallas kernels  186 us (96%)
  local copies, waits for them, and re-layouts  6.35 us (3%)
    pallas_call x1, Pallas kernels, on_device(): pl.pallas_call(kernel, out_shape=(jax.ShapeDtypeStruct((1, TOK, D), bf),...  186 us
    unnamed x13, local copies, waits for them, and re-layouts  6.35 us

profile of v3, /device:TPU:0, one launch (start us, length us, event | category | flops | bytes accessed | tf_op | source)
XLA Modules:
  0.0 193.1 jit_solution(14482558792963301617)
XLA Ops:
  0.6 186.1 %shard_map.128 = (bf16[1,128,8192]{2,1,0:T(8,128)(2,1)}, bf16[1,128,4096]{2,1,0:T(8,128)(2,1)}, f32[1,256,512]{2,1,0:T(8,128)}, f32[1,256,512]{2,1,0:T(8,128)}, f32[1,256]{1,0:T(1,128)}) custom-call(s32[1,2,2,4]{3,2,1,0:T(2,128)} %exps.1, s32[64]{0:T(128)} %docs.1, bf16[1,128,8192]{2,1,0:T(8,128)(2,1)} %x.1, bf16[1,128,4096]{2,1,0:T(8,128)(2,1)} %q.1, ...), custom_call_target="tpu_custom_call" | custom-call | tf_op jit(solution)/shard_map/pallas_call | solution.py:641
  186.7 0.0 copy-start
  186.7 0.0 copy-start.2
  186.7 3.2 %copy.19 = bf16[1,128,8192]{2,1,0:T(8,128)(2,1)} copy(bf16[1,128,8192]{2,1,0:T(8,128)(2,1)} %get-tuple-element.10) | data formatting | bytes 4194304
  189.9 0.0 copy-done
  189.9 0.0 copy-start.1
  190.0 0.0 copy-start.3
  190.0 1.0 copy.20
  190.9 0.0 copy-done.2
  190.9 0.8 copy.21
  191.7 0.0 copy-done.1
  191.7 0.8 copy.22
  192.5 0.0 copy-done.3
  192.5 0.6 copy.23
Async XLA Ops:
  186.7 3.2 %copy-start = (bf16[1,128,4096]{2,1,0:T(8,128)(2,1)S(1)}, bf16[1,128,4096]{2,1,0:T(8,128)(2,1)}, u32[]{:S(2)}) copy-start(bf16[1,128,4096]{2,1,0:T(8,128)(2,1)} %get-tuple-element.11) | copy-start | bytes 3145732
  186.7 4.2 %copy-start.2 = (f32[1,256,512]{2,1,0:T(8,128)S(1)}, f32[1,256,512]{2,1,0:T(8,128)}, u32[]{:S(2)}) copy-start(f32[1,256,512]{2,1,0:T(8,128)} %get-tuple-element.12) | copy-start | bytes 1572868
  189.9 1.8 copy-start.1
  190.0 2.6 %copy-start.3 = (f32[1,256]{1,0:T(1,128)S(1)}, f32[1,256]{1,0:T(1,128)}, u32[]{:S(2)}) copy-start(f32[1,256]{1,0:T(1,128)} %get-tuple-element.14) | copy-start | bytes 3076

commit v4 on v3

--- a/solution.py
+++ b/solution.py
@@ -27,6 +27,7 @@
 SLAB = 1024
 WIN = (REACH + 1) * TOK
 PAIR = 2
+ORDER = (0, 2, 6, 4, 3, 5, 1, 7)
 
 MESH = pl.DeviceIdType.MESH
 NT = (((1,), (1,)), ((), ()))
@@ -412,31 +413,78 @@
                 if c < 2:
                     total = rope(total, -1.0)
                 gall[half_slab(u, 0), slab(c)] = total.astype(jnp.bfloat16)
-            for k in range(1, F):
-                ga_copy(u, k).start()
+            gathers[u].first()
 
         def sent(self):
             for copy in (self.a, self.b, self.c, self.d):
                 copy.wait_send()
 
-    def ga_copy(u, k):
-        return rcopy(gall.at[half_slab(u, 0)], gall.at[half_slab(u, k)],
-                     sga.at[u * F + k], rga.at[u * F + k], f_up(k))
+    class Gather:
+        def __init__(self, u):
+            def copy(src, dst_slot, n, dev):
+                return rcopy(gall.at[half_slab(u, src)], gall.at[half_slab(u, dst_slot)],
+                             sga.at[u * F + n], rga.at[u * F + dst_slot], dev)
+
+            mates = range(2, F, 2)
+            self.column = [copy(0, k, k, f_up(k)) for k in mates]
+            self.even_side = copy(0, 1, 7, f_up(1))
+            self.odd_side = copy(0, 7, 7, f_up(7))
+            self.even_on = [copy(7, k - 1, k - 1, f_up(k)) for k in mates]
+            self.odd_on = [copy(1, k + 1, k - 1, f_up(k)) for k in mates]
+            self.into = [copy(0, k, 0, f_up(k)) for k in range(1, F)]
+
+        def first(self):
+            @pl.when(xl == 0)
+            def _():
+                self.even_side.start()
+
+            @pl.when(xl == 1)
+            def _():
+                self.odd_side.start()
+
+            for member in self.column:
+                member.start()
+
+        def second(self):
+            @pl.when(xl == 0)
+            def _():
+                self.into[6].wait_recv()
+                for member in self.even_on:
+                    member.start()
+
+            @pl.when(xl == 1)
+            def _():
+                self.into[0].wait_recv()
+                for member in self.odd_on:
+                    member.start()
+
+        def arrived(self, k):
+            if 1 < k < 7:
+                self.into[k - 1].wait_recv()
+            else:
+                @pl.when(xl == (0 if k == 1 else 1))
+                def _():
+                    self.into[k - 1].wait_recv()
+
+        def sent(self):
+            for member in self.column + [self.even_side] + self.even_on:
+                member.wait_send()
 
     windows = [Window(0), Window(1)]
     terms = [Terms(0), Terms(1)]
+    gathers = [Gather(0), Gather(1)]
     own_block(0)
     windows[0].first()
     pltpu.make_async_copy(qs, qs, lsem.at[3]).wait()
     pltpu.make_async_copy(dos, dos, lsem.at[4]).wait()
     windows[0].second()
     windows[0].third()
+    windows[0].last()
+    attend(0, 0, steps // 2)
     own_block(1)
     windows[1].first()
-    windows[0].last()
-    attend(0, 0, steps // 2)
+    attend(0, steps // 2, steps)
     windows[1].second()
-    attend(0, steps // 2, steps)
     attend(1, 0, steps // 2)
     windows[1].third()
     attend(1, steps // 2, steps)
@@ -452,6 +500,7 @@
     out_q.start()
     terms[0].last()
     terms[1].second()
+    gathers[0].second()
     terms[1].third()
     terms[1].last()
 
@@ -469,10 +518,12 @@
     def h_copy(k):
         return rcopy(hgs.at[slab(k)], sgr.at[slab(k)], sh.at[k], rh.at[k], f_down(k))
 
-    for k in range(F):
+    for place, k in enumerate(ORDER):
         if k > 0:
-            ga_copy(0, k).wait_recv()
-            ga_copy(1, k).wait_recv()
+            if place == 1:
+                gathers[1].second()
+            gathers[0].arrived(k)
+            gathers[1].arrived(k)
         hg = (dot(gall[half_slab(0, k), :], wr[:, 0:KVW], NT)
               + dot(gall[half_slab(1, k), :], wr[:, KVW:], NT))
         scaled = (hg * gain_row).astype(jnp.bfloat16)
@@ -517,7 +568,7 @@
         part = slab(n, T)
         return rcopy(cout.at[part], cin.at[part], src_.at[n], rrc.at[n], ((p + 3) % 4, i))
 
-    for n in range(F):
+    for place, n in enumerate(ORDER):
         if n > 0:
             h_copy(n).wait_recv()
 
@@ -539,8 +590,8 @@
         for m in range(T):
             pltpu.make_async_copy(
                 cout.at[n * T + m], o_in.at[0, :, x_cols(n * T + m)], osem.at[1]).start()
-        if n < T:
-            weight_term((n + 1) % T)
+        if place < T:
+            weight_term((place + 1) % T)
 
     for k in range(1, T):
         ws_copy(k).wait_recv()
@@ -566,14 +617,13 @@
         r_copy(k).wait_send()
         for u in range(2):
             p_copy(u, k).wait_send()
-            ga_copy(u, k).wait_send()
         h_copy(k).wait_send()
     for k in range(1, T):
         w_copy(k).wait_send()
         g_copy(k).wait_send()
         ws_copy(k).wait_send()
         gs_copy(k).wait_send()
-    for member in windows + terms:
+    for member in windows + terms + gathers:
         member.sent()
 
     @pl.when(p > 0)
@@ -583,6 +633,21 @@
 
     pltpu.make_async_copy(cout, cout, osem.at[1]).wait()
     for copy in [out_q] + outs:
+        copy.wait()
+
+
+def hand_on(in_in, in_q, in_kw, in_vw, in_gain, o_in, o_q, o_kw, o_vw, o_gain, sem):
+    copies = []
+    for src, dst, parts in ((in_in, o_in, 4), (in_q, o_q, 2), (in_kw, o_kw, 2), (in_vw, o_vw, 2)):
+        size = src.shape[1] // parts
+        for n in range(parts):
+            part = slice(n * size, (n + 1) * size)
+            copies.append(pltpu.make_async_copy(
+                src.at[0, part], dst.at[0, part], sem.at[len(copies)]))
+    copies.append(pltpu.make_async_copy(in_gain, o_gain, sem.at[len(copies)]))
+    for copy in copies:
+        copy.start()
+    for copy in copies:
         copy.wait()
 
 
@@ -654,7 +719,14 @@
             collective_id=0, has_side_effects=True, vmem_limit_bytes=60 * 1024 * 1024),
     )(weight_exponents, doc_lengths, layer_input, queries, out_grad, top_grad, norm_gain,
       key_weight, value_weight)
-    return o_in, o_q, o_kw, o_vw, o_gain
+    results = (o_in, o_q, o_kw, o_vw, o_gain)
+    return pl.pallas_call(
+        hand_on,
+        out_shape=tuple(jax.ShapeDtypeStruct(r.shape, r.dtype) for r in results),
+        in_specs=[hbm] * 5,
+        out_specs=(hbm,) * 5,
+        scratch_shapes=[dma((11,))],
+    )(*results)
 
 
 def solution(mesh):

time: 193 us -> 319 us (1.65)
  Pallas kernels: 186 us -> 317 us
  local copies, waits for them, and re-layouts: 6.35 us -> 0 us
    pallas_call x0 -> x1, Pallas kernels: none -> 128 us  [on_device(): pl.pallas_call(hand_on, out_shape=tuple((jax.ShapeDtypeStruct(r.shape, r....]
    unnamed x13 -> x0, local copies, waits for them, and re-layouts: 6.35 us -> none
where the time goes in v4:
time: 319 us; the launch traced here: 318 us
  Pallas kernels  317 us (99%)
    pallas_call x1, Pallas kernels, on_device(): pl.pallas_call(kernel, out_shape=(jax.ShapeDtypeStruct((1, TOK, D), bf),...  189 us
    pallas_call x1, Pallas kernels, on_device(): pl.pallas_call(hand_on, out_shape=tuple((jax.ShapeDtypeStruct(r.shape, r....  128 us

profile of v4, /device:TPU:0, one launch (start us, length us, event | category | flops | bytes accessed | tf_op | source)
XLA Modules:
  0.0 318.1 jit_solution(239617753272922774)
XLA Ops:
  0.6 189.0 %shard_map.128 = (bf16[1,128,8192]{2,1,0:T(8,128)(2,1)}, bf16[1,128,4096]{2,1,0:T(8,128)(2,1)}, f32[1,256,512]{2,1,0:T(8,128)}, f32[1,256,512]{2,1,0:T(8,128)}, f32[1,256]{1,0:T(1,128)}) custom-call(s32[1,2,2,4]{3,2,1,0:T(2,128)} %exps.1, s32[64]{0:T(128)} %docs.1, bf16[1,128,8192]{2,1,0:T(8,128)(2,1)} %x.1, bf16[1,128,4096]{2,1,0:T(8,128)(2,1)} %q.1, ...), custom_call_target="tpu_custom_call" | custom-call | tf_op jit(solution)/shard_map/pallas_call | solution.py:706
  189.6 128.3 %shard_map.129 = (bf16[1,128,8192]{2,1,0:T(8,128)(2,1)}, bf16[1,128,4096]{2,1,0:T(8,128)(2,1)}, f32[1,256,512]{2,1,0:T(8,128)}, f32[1,256,512]{2,1,0:T(8,128)}, f32[1,256]{1,0:T(1,128)}) custom-call(bf16[1,128,8192]{2,1,0:T(8,128)(2,1)} %get-tuple-element.10.in_in, bf16[1,128,4096]{2,1,0:T(8,128)(2,1)} %get-tuple-element.11.in_q, ...), custom_call_target="tpu_custom_call" | custom-call | tf_op jit(solution)/shard_map/pallas_call | solution.py:723

commit v5 on v3

--- a/solution.py
+++ b/solution.py
@@ -26,7 +26,9 @@
 T = 4
 SLAB = 1024
 WIN = (REACH + 1) * TOK
-PAIR = 2
+PAIR = 4
+PARTS = 4
+ORDER = (0, 1, 2, 3, 4, 5, 6, 7)
 
 MESH = pl.DeviceIdType.MESH
 NT = (((1,), (1,)), ((), ()))
@@ -412,19 +414,32 @@
                 if c < 2:
                     total = rope(total, -1.0)
                 gall[half_slab(u, 0), slab(c)] = total.astype(jnp.bfloat16)
-            for k in range(1, F):
-                ga_copy(u, k).start()
+            gathers[u].first()
 
         def sent(self):
             for copy in (self.a, self.b, self.c, self.d):
                 copy.wait_send()
 
-    def ga_copy(u, k):
-        return rcopy(gall.at[half_slab(u, 0)], gall.at[half_slab(u, k)],
-                     sga.at[u * F + k], rga.at[u * F + k], f_up(k))
+    class Gather:
+        def __init__(self, u):
+            self.copies = [rcopy(gall.at[half_slab(u, 0)], gall.at[half_slab(u, k)],
+                                 sga.at[u * F + k], rga.at[u * F + k], f_up(k))
+                           for k in range(1, F)]
+
+        def first(self):
+            for copy in self.copies:
+                copy.start()
+
+        def arrived(self, k):
+            self.copies[k - 1].wait_recv()
+
+        def sent(self):
+            for copy in self.copies:
+                copy.wait_send()
 
     windows = [Window(0), Window(1)]
     terms = [Terms(0), Terms(1)]
+    gathers = [Gather(0), Gather(1)]
     own_block(0)
     windows[0].first()
     pltpu.make_async_copy(qs, qs, lsem.at[3]).wait()
@@ -469,10 +484,10 @@
     def h_copy(k):
         return rcopy(hgs.at[slab(k)], sgr.at[slab(k)], sh.at[k], rh.at[k], f_down(k))
 
-    for k in range(F):
+    for place, k in enumerate(ORDER):
         if k > 0:
-            ga_copy(0, k).wait_recv()
-            ga_copy(1, k).wait_recv()
+            gathers[0].arrived(k)
+            gathers[1].arrived(k)
         hg = (dot(gall[half_slab(0, k), :], wr[:, 0:KVW], NT)
               + dot(gall[half_slab(1, k), :], wr[:, KVW:], NT))
         scaled = (hg * gain_row).astype(jnp.bfloat16)
@@ -517,7 +532,7 @@
         part = slab(n, T)
         return rcopy(cout.at[part], cin.at[part], src_.at[n], rrc.at[n], ((p + 3) % 4, i))
 
-    for n in range(F):
+    for place, n in enumerate(ORDER):
         if n > 0:
             h_copy(n).wait_recv()
 
@@ -539,8 +554,9 @@
         for m in range(T):
             pltpu.make_async_copy(
                 cout.at[n * T + m], o_in.at[0, :, x_cols(n * T + m)], osem.at[1]).start()
-        if n < T:
-            weight_term((n + 1) % T)
+        if place == 0:
+            for part in (1, 2, 3, 0):
+                weight_term(part)
 
     for k in range(1, T):
         ws_copy(k).wait_recv()
@@ -566,14 +582,13 @@
         r_copy(k).wait_send()
         for u in range(2):
             p_copy(u, k).wait_send()
-            ga_copy(u, k).wait_send()
         h_copy(k).wait_send()
     for k in range(1, T):
         w_copy(k).wait_send()
         g_copy(k).wait_send()
         ws_copy(k).wait_send()
         gs_copy(k).wait_send()
-    for member in windows + terms:
+    for member in windows + terms + gathers:
         member.sent()
 
     @pl.when(p > 0)
@@ -584,6 +599,11 @@
     pltpu.make_async_copy(cout, cout, osem.at[1]).wait()
     for copy in [out_q] + outs:
         copy.wait()
+
+
+def hand_on(in_in, in_q, in_kw, in_vw, in_gain, o_in, o_q, o_kw, o_vw, o_gain):
+    for src, dst in ((in_in, o_in), (in_q, o_q), (in_kw, o_kw), (in_vw, o_vw), (in_gain, o_gain)):
+        dst[...] = src[...]
 
 
 def on_device(layer_input, queries, out_grad, top_grad, norm_gain, key_weight, value_weight,
@@ -654,7 +674,17 @@
             collective_id=0, has_side_effects=True, vmem_limit_bytes=60 * 1024 * 1024),
     )(weight_exponents, doc_lengths, layer_input, queries, out_grad, top_grad, norm_gain,
       key_weight, value_weight)
-    return o_in, o_q, o_kw, o_vw, o_gain
+    results = (o_in, o_q, o_kw, o_vw, o_gain)
+    blocks = [pl.BlockSpec((1, r.shape[1] // PARTS, r.shape[2]), lambda n: (0, n, 0))
+              for r in results[:4]]
+    blocks.append(pl.BlockSpec((1, ROWS), lambda n: (0, 0)))
+    return pl.pallas_call(
+        hand_on,
+        out_shape=tuple(jax.ShapeDtypeStruct(r.shape, r.dtype) for r in results),
+        grid=(PARTS,),
+        in_specs=blocks,
+        out_specs=tuple(blocks),
+    )(*results)
 
 
 def solution(mesh):

time: 193 us -> 188 us (0.974)
  local copies, waits for them, and re-layouts: 6.35 us -> 0 us
    unnamed x13 -> x0, local copies, waits for them, and re-layouts: 6.35 us -> none
    pallas_call x1, Pallas kernels: 186 us -> 181 us  [on_device(): pl.pallas_call(kernel, out_shape=(jax.ShapeDtypeStruct((1, TOK, D), bf),...]
    pallas_call x0 -> x1, Pallas kernels: none -> 4.66 us  [on_device(): pl.pallas_call(hand_on, out_shape=tuple((jax.ShapeDtypeStruct(r.shape, r....]
where the time goes in v5:
time: 188 us; the launch traced here: 187 us
  Pallas kernels  186 us (99%)
    pallas_call x1, Pallas kernels, on_device(): pl.pallas_call(kernel, out_shape=(jax.ShapeDtypeStruct((1, TOK, D), bf),...  181 us
    pallas_call x1, Pallas kernels, on_device(): pl.pallas_call(hand_on, out_shape=tuple((jax.ShapeDtypeStruct(r.shape, r....  4.66 us

profile of v5, /device:TPU:0, one launch (start us, length us, event | category | flops | bytes accessed | tf_op | source)
XLA Modules:
  0.0 186.7 jit_solution(5603547492121176184)
XLA Ops:
  0.6 181.2 %shard_map.128 = (bf16[1,128,8192]{2,1,0:T(8,128)(2,1)}, bf16[1,128,4096]{2,1,0:T(8,128)(2,1)}, f32[1,256,512]{2,1,0:T(8,128)}, f32[1,256,512]{2,1,0:T(8,128)}, f32[1,256]{1,0:T(1,128)}) custom-call(s32[1,2,2,4]{3,2,1,0:T(2,128)} %exps.1, s32[64]{0:T(128)} %docs.1, bf16[1,128,8192]{2,1,0:T(8,128)(2,1)} %x.1, bf16[1,128,4096]{2,1,0:T(8,128)(2,1)} %q.1, ...), custom_call_target="tpu_custom_call" | custom-call | tf_op jit(solution)/shard_map/pallas_call | solution.py:661
  181.9 4.7 %shard_map.129 = (bf16[1,128,8192]{2,1,0:T(8,128)(2,1)}, bf16[1,128,4096]{2,1,0:T(8,128)(2,1)}, f32[1,256,512]{2,1,0:T(8,128)}, f32[1,256,512]{2,1,0:T(8,128)}, f32[1,256]{1,0:T(1,128)}) custom-call(bf16[1,128,8192]{2,1,0:T(8,128)(2,1)} %get-tuple-element.10.in_in, bf16[1,128,4096]{2,1,0:T(8,128)(2,1)} %get-tuple-element.11.in_q, ...), custom_call_target="tpu_custom_call" | custom-call | tf_op jit(solution)/shard_map/pallas_call | solution.py:681

commit v6 on v5

--- a/solution.py
+++ b/solution.py
@@ -233,20 +233,25 @@
         return rcopy(psend.at[half_slab(u, k)], precv.at[half_slab(u, k)],
                      sp.at[u * F + k], rp.at[u * F + k], f_down(k))
 
+    def product(u, g):
+        part = dot(hbuf[slab(g, 2 * TOK), :], wr[:, slab(u, KVW)]).astype(jnp.bfloat16)
+        for n in range(2):
+            k = 2 * g + n
+            target = psend if k > 0 else precv
+            target[half_slab(u, k), :] = part[slab(n), :]
+            if k > 0:
+                p_copy(u, k).start()
+
     for k in range(F):
         if k > 0:
             x_copy(k).wait_recv()
             r_copy(k).wait_recv()
         hidden = (slab_x(k) * wide(inv_rms(k), SLAB) * gain_row).astype(jnp.bfloat16)
         hbuf[slab(k), :] = hidden
-        part = dot(hidden, wr[...]).astype(jnp.bfloat16)
-        for u in range(2):
-            target = psend if k > 0 else precv
-            target[half_slab(u, k), :] = part[:, slab(u, KVW)]
-        if k > 0:
-            p_copy(0, k).start()
-    for k in range(1, F):
-        p_copy(1, k).start()
+        if k % 2 == 1:
+            product(0, k // 2)
+    for g in range(F // 2):
+        product(1, g)
 
     for k in range(F):
         ht[:, slab(k)] = hbuf[slab(k), :].T

time: 188 us -> 186 us (0.989)
  Pallas kernels: 186 us -> 184 us
where the time goes in v6:
time: 186 us; the launch traced here: 185 us
  Pallas kernels  184 us (99%)
    pallas_call x1, Pallas kernels, on_device(): pl.pallas_call(kernel, out_shape=(jax.ShapeDtypeStruct((1, TOK, D), bf),...  179 us
    pallas_call x1, Pallas kernels, on_device(): pl.pallas_call(hand_on, out_shape=tuple((jax.ShapeDtypeStruct(r.shape, r....  4.66 us

profile of v6, /device:TPU:0, one launch (start us, length us, event | category | flops | bytes accessed | tf_op | source)
XLA Modules:
  0.0 184.9 jit_solution(10834836027935517082)
XLA Ops:
  0.6 179.4 %shard_map.128 = (bf16[1,128,8192]{2,1,0:T(8,128)(2,1)}, bf16[1,128,4096]{2,1,0:T(8,128)(2,1)}, f32[1,256,512]{2,1,0:T(8,128)}, f32[1,256,512]{2,1,0:T(8,128)}, f32[1,256]{1,0:T(1,128)}) custom-call(s32[1,2,2,4]{3,2,1,0:T(2,128)} %exps.1, s32[64]{0:T(128)} %docs.1, bf16[1,128,8192]{2,1,0:T(8,128)(2,1)} %x.1, bf16[1,128,4096]{2,1,0:T(8,128)(2,1)} %q.1, ...), custom_call_target="tpu_custom_call" | custom-call | tf_op jit(solution)/shard_map/pallas_call | solution.py:666
  180.1 4.7 %shard_map.129 = (bf16[1,128,8192]{2,1,0:T(8,128)(2,1)}, bf16[1,128,4096]{2,1,0:T(8,128)(2,1)}, f32[1,256,512]{2,1,0:T(8,128)}, f32[1,256,512]{2,1,0:T(8,128)}, f32[1,256]{1,0:T(1,128)}) custom-call(bf16[1,128,8192]{2,1,0:T(8,128)(2,1)} %get-tuple-element.10.in_in, bf16[1,128,4096]{2,1,0:T(8,128)(2,1)} %get-tuple-element.11.in_q, ...), custom_call_target="tpu_custom_call" | custom-call | tf_op jit(solution)/shard_map/pallas_call | solution.py:686
